TPU v7x, 128 devices: a whole 4x4x4 slice. The times are simulated.
128 devices in a mesh: feed: 16 (over z, y_hi, core), chan: 8 (over x, y_lo).
Axes of the slice: x: 4, y: 4 (y_hi: 2, y_lo: 2; y = y_hi * 2 + y_lo), z: 4, core: 2. Of those that a mesh axis runs over, the one named last changes fastest.
Arguments:
- raw_samples: bfloat16 [256, 90112], P(('feed', 'chan')), may hold values from -6 to 6
- stack_code: int32 [256, 256], P('feed'), may hold values from -382 to 381, as said below
- stack_owner: int32 [382], replicated, may hold values from 0 to 15, as said below
Outputs:
- visibilities: float32 [752, 2, 2048], P('feed', None, 'chan')
Inputs may be any that keep to these rules, and one draw needn't show every extreme that they name: `stack_code`: entry [i, j] names the stack of the baseline from input i to input j: s when it has stack s's orientation, -1 - s when reversed. For i != j entry [j, i] is -1 minus entry [i, j]; the diagonal holds 0; every stack is named. `stack_owner`: no owner has more than 47 stacks, and one owner has exactly 47.
All inputs are finite; a program needn't handle non-finite values.
Results may differ from a plain program's by a relative error of at most 0.0083.
Values may be sent and summed in bfloat16 or wider, within the bound.
A program may use at most 64 MiB of HBM per device.

v0:
```python
import math

import numpy as np
import jax
import jax.numpy as jnp
from jax import lax
from jax.experimental import pallas as pl
from jax.experimental.pallas import tpu as pltpu
from jax.sharding import PartitionSpec as P

SPECTRA = 4
TAPS = 8
FA = 64
FB = 128
FRAME = 8192
STACKS = 382
CAP = 47
FEEDS = 16
GROUPS = 8
INPUTS = 256
HALF = 128
CHUNK = 8
NB = 3
F32 = jnp.float32
BF16 = jnp.bfloat16
NT = (((1,), (1,)), ((), ()))


def window_table():
    length = TAPS * FRAME
    sample = np.arange(length, dtype=np.float64)
    centred = (sample - length / 2 + 0.5) / FRAME
    weights = np.sinc(centred) * (0.5 - 0.5 * np.cos(2.0 * np.pi * (sample + 0.5) / length))
    weights = weights * np.sqrt(FRAME / np.sum(weights * weights))
    return weights.reshape(TAPS, FA, FB).astype(np.float32)


def turns(left, right, modulus):
    return 2.0 * np.pi * (np.outer(left, right) % modulus) / modulus


def first_matrix():
    angles = turns(np.arange(FA), np.arange(FA), FA)
    parts = np.stack([np.cos(angles), -np.sin(angles)]).reshape(2, FA, 4, 16)
    out = np.zeros((2, 4, 2, 16, FA, 2), np.float32)
    for i in range(2):
        out[:, :, i, :, :, i] = parts.transpose(0, 2, 3, 1)
    return out.reshape(256, 128)


def twiddle_tables():
    angles = turns(np.arange(FA), np.arange(FB), FRAME).reshape(4, 1, 16, FB)
    angles = np.broadcast_to(angles, (4, 2, 16, FB)).reshape(128, FB)
    return np.stack([np.cos(angles), np.sin(angles)]).astype(np.float32)


def second_matrix():
    angles = turns(np.arange(32), np.arange(FB), FB)
    return np.concatenate([np.cos(angles), np.sin(angles)], axis=1).astype(np.float32)


def bf(table):
    return jnp.asarray(table).astype(BF16)


def channelize(x_ref, win_ref, first_ref, tw_ref, second_ref, mixed_ref, wide_ref):
    frames = []
    for t in range(SPECTRA):
        total = jnp.zeros((128, FB), F32)
        for p in range(TAPS):
            rows = x_ref[pl.ds((t + p) * 128, 128), :].astype(F32)
            total = total + win_ref[p] * rows
        frames.append(total.astype(BF16))
    frames = jnp.concatenate(frames, axis=1)
    section = jnp.dot(first_ref[...], frames, preferred_element_type=F32)
    cosine, sine = tw_ref[0], tw_ref[1]
    for t in range(SPECTRA):
        re = section[:128, t * FB : (t + 1) * FB]
        im = section[128:, t * FB : (t + 1) * FB]
        real = re * cosine + im * sine
        imag = im * cosine - re * sine
        minus = (-real).astype(BF16)
        real = real.astype(BF16)
        imag = imag.astype(BF16)
        for u in range(8):
            rows = slice(u * 16, u * 16 + 16)
            base = (u * 8 + t) * 16
            mixed_ref[base : base + 16, :FB] = real[rows]
            mixed_ref[base : base + 16, FB:] = imag[rows]
            base = (u * 8 + 4 + t) * 16
            mixed_ref[base : base + 16, :FB] = imag[rows]
            mixed_ref[base : base + 16, FB:] = minus[rows]
    out = lax.dot_general(second_ref[...], mixed_ref[...], NT, preferred_element_type=F32)
    out = out * (1.0 / math.sqrt(FRAME))
    for u in range(8):
        wide_ref[pl.ds(u, 32, stride=8), :] = out[:, u * 128 : (u + 1) * 128]
    return wide_ref[...].astype(BF16)


def regroup(block):
    row = lax.broadcasted_iota(jnp.int32, (256, 256), 0)
    col = lax.broadcasted_iota(jnp.int32, (256, 256), 1)
    source = ((row // 2) % 8) * 32 + (row // 16) * 2 + row % 2
    take = jnp.where(col == source, 1.0, 0.0).astype(BF16)
    return jnp.dot(take, block, preferred_element_type=F32).astype(BF16)


def stack_pairs(x_ref, code_ref, xf_ref, left_ref, right_ref, data_ref, hot_ref, acc_ref):
    x = x_ref[...]
    xf = x.astype(F32)
    xf_ref[0] = xf
    xf_ref[1] = jnp.concatenate([xf[:, 64:], -xf[:, :64]], axis=1)
    acc_ref[...] = jnp.zeros_like(acc_ref)
    lane = lax.broadcasted_iota(jnp.int32, (16, 128), 1)
    sub = lax.broadcasted_iota(jnp.int32, (16, 128), 0)
    pick = lane % 16 == sub
    hot_row = lax.broadcasted_iota(jnp.int32, (128, INPUTS), 0)
    lane_j = lax.broadcasted_iota(jnp.int32, (32, 128), 1)
    bid = lax.broadcasted_iota(jnp.int32, (16, INPUTS), 0)

    @pl.loop(0, HALF // CHUNK)
    def _(step):
        base = step * CHUNK
        for n in range(CHUNK):
            for q in range(2):
                at = slice(n * 32 + q * 16, n * 32 + q * 16 + 16)
                row = xf_ref[q, pl.ds(base + n, 1), :]
                left_ref[at, :] = jnp.where(pick, row, 0.0).astype(BF16)
                row = xf_ref[q, pl.ds(HALF + base + n, 1), :]
                right_ref[at, :] = jnp.where(pick, row, 0.0).astype(BF16)
        one = lax.dot_general(left_ref[...], x_ref[...], NT, preferred_element_type=F32)
        two = lax.dot_general(right_ref[...], x_ref[HALF:, :], NT, preferred_element_type=F32)
        for n in range(CHUNK):
            at = slice(n * 32, n * 32 + 32)
            low = jnp.where(lane_j > base + n, one[at, :128], two[at, :])
            both = jnp.concatenate([low, one[at, 128:]], axis=1)
            code = code_ref[pl.ds(base + n, 1), :]
            target = jnp.where(code >= 0, code, -1 - code)
            sign = jnp.where(code >= 0, 1.0, -1.0).astype(F32)
            used = lax.broadcasted_iota(jnp.int32, (1, INPUTS), 1) != base + n
            hi = target // 128
            lo = jnp.where(used, target % 128, -1)
            real = both[:16].astype(BF16)
            imag = (both[16:] * sign).astype(BF16)
            lanes = slice(n * INPUTS, (n + 1) * INPUTS)
            zero = jnp.zeros((), BF16)
            for b in range(NB):
                data_ref[b * 32 : b * 32 + 16, lanes] = jnp.where(hi == b, real, zero)
                data_ref[b * 32 + 16 : b * 32 + 32, lanes] = jnp.where(hi == b, imag, zero)
            data_ref[NB * 32 : NB * 32 + 16, lanes] = jnp.where(hi == bid, 1.0, 0.0).astype(BF16)
            hot_ref[:, lanes] = jnp.where(hot_row == lo, 1.0, 0.0).astype(BF16)
        acc_ref[...] += lax.dot_general(data_ref[...], hot_ref[...], NT, preferred_element_type=F32)


def messages(acc_ref, owner_ref):
    owner = owner_ref[...]
    wide = jnp.broadcast_to(owner, (128, NB * 128))
    tall = jnp.transpose(wide.astype(F32))
    rank = jnp.zeros((1, NB * 128), F32)
    cols = []
    for b in range(NB):
        mine = owner[:, b * 128 : (b + 1) * 128].astype(F32)
        row = lax.broadcasted_iota(jnp.int32, (NB * 128, 128), 0)
        col = lax.broadcasted_iota(jnp.int32, (NB * 128, 128), 1) + b * 128
        same = jnp.where((tall == mine) & (row < col), 1.0, 0.0)
        cols.append(jnp.sum(same, axis=0, keepdims=True))
    rank = jnp.concatenate(cols, axis=1).astype(jnp.int32)
    place = jnp.where(owner >= 0, owner * 128 + rank, -1)
    slot = lax.broadcasted_iota(jnp.int32, (FEEDS * 128, NB * 128), 0)
    perm_re = jnp.where(slot == place, 1.0, 0.0).astype(BF16)
    perm_im = jnp.where(slot == jnp.where(owner >= 0, place + 64, -1), 1.0, 0.0).astype(BF16)
    perm = jnp.concatenate([perm_re, perm_im], axis=1)
    parts = []
    for q in range(2):
        for b in range(NB):
            sums = acc_ref[b * 32 + q * 16 : b * 32 + q * 16 + 16, :]
            count = acc_ref[NB * 32 + b : NB * 32 + b + 1, :]
            parts.append(sums / jnp.maximum(count, 1.0))
    means = jnp.concatenate(parts, axis=1)
    high = means.astype(BF16)
    low = (means - high.astype(F32)).astype(BF16)
    both = jnp.concatenate([high, low], axis=0)
    out = lax.dot_general(both, perm, NT, preferred_element_type=F32)
    return out[:16] + out[16:]


def finish(block, out_ref):
    turned = jnp.transpose(block)
    out_ref[:, 0, :] = turned[:CAP]
    out_ref[:, 1, :] = turned[64 : 64 + CAP]


def k_channelize(x_ref, win_ref, first_ref, tw_ref, second_ref, out_ref, mixed_ref, wide_ref):
    out_ref[...] = channelize(x_ref, win_ref, first_ref, tw_ref, second_ref, mixed_ref, wide_ref)


def k_regroup(in_ref, out_ref):
    out_ref[...] = regroup(in_ref[...])


def k_stack(x_ref, code_ref, owner_ref, out_ref, xf, left, right, data, hot, acc):
    stack_pairs(x_ref, code_ref, xf, left, right, data, hot, acc)
    out = messages(acc, owner_ref)
    for o in range(FEEDS):
        out_ref[o] = out[:, o * 128 : (o + 1) * 128]


def k_finish(in_ref, out_ref):
    finish(in_ref[...], out_ref)


def call(kernel, shape, dtype, scratch, *args):
    return pl.pallas_call(
        kernel,
        out_shape=jax.ShapeDtypeStruct(shape, dtype),
        in_specs=[pl.BlockSpec(memory_space=pltpu.VMEM)] * len(args),
        out_specs=pl.BlockSpec(memory_space=pltpu.VMEM),
        scratch_shapes=scratch,
        compiler_params=pltpu.CompilerParams(vmem_limit_bytes=60 << 20),
    )(*args)


def fold_codes(codes):
    row = lax.broadcasted_iota(jnp.int32, (HALF, HALF), 0)
    col = lax.broadcasted_iota(jnp.int32, (HALF, HALF), 1)
    low = jnp.where(col > row, codes[:HALF, :HALF], codes[HALF:, HALF:])
    return jnp.concatenate([low, codes[:HALF, HALF:]], axis=1)


def per_device(raw_samples, stack_code, stack_owner):
    x = raw_samples.reshape(2, 704, 128).transpose(1, 0, 2).reshape(1408, 128)
    win = jnp.asarray(np.repeat(window_table(), 2, axis=1))
    wide = call(
        k_channelize, (256, 128), BF16,
        [pltpu.VMEM((1024, 256), BF16), pltpu.VMEM((256, 128), F32)],
        x, win, bf(first_matrix()), jnp.asarray(twiddle_tables()), bf(second_matrix()),
    )
    got = lax.all_to_all(wide.reshape(8, 32, 128), "chan", 0, 0, tiled=True)
    regrouped = call(k_regroup, (256, 128), BF16, [], got.reshape(256, 128))
    spectra = lax.all_to_all(regrouped.reshape(16, 16, 128), "feed", 0, 0, tiled=True)
    codes = fold_codes(lax.all_gather(stack_code, "feed", axis=0, tiled=True))
    owner = jnp.pad(stack_owner, (0, 2), constant_values=-1).reshape(1, NB * 128)
    msgs = call(
        k_stack, (16, 16, 128), F32,
        [
            pltpu.VMEM((2, 256, 128), F32),
            pltpu.VMEM((CHUNK * 32, 128), BF16),
            pltpu.VMEM((CHUNK * 32, 128), BF16),
            pltpu.VMEM((NB * 32 + 16, CHUNK * 256), BF16),
            pltpu.VMEM((128, CHUNK * 256), BF16),
            pltpu.VMEM((NB * 32 + 16, 128), F32),
        ],
        spectra.reshape(256, 128), codes, owner,
    )
    back = lax.all_to_all(msgs, "feed", 0, 0, tiled=True)
    return call(k_finish, (CAP, 2, 256), F32, [], back.reshape(256, 128))


def solution(mesh):
    placed = (P(("feed", "chan"), None), P("feed", None), P())
    return jax.shard_map(
        per_device, mesh=mesh, in_specs=placed, out_specs=P("feed", None, "chan"), check_vma=False
    )
```

profile of v0, /device:TPU:1, one launch (start us, length us, event | category | flops | bytes accessed | tf_op | source)
XLA Modules:
  0.0 75.1 jit_solution(10053163154791352914)
XLA Ops:
  0.0 2.4 %shard_map.73 = bf16[256,128]{1,0:T(8,128)(2,1)} custom-call(bf16[1408,128]{1,0:T(8,128)(2,1)} %bitcast.11, f32[8,128,128]{2,1,0:T(8,128)} %constant.10.clone.win_ref, bf16[256,128]{1,0:T(8,128)(2,1)} %constant.17.first_ref, f32[2,128,128]{2,1,0:T(8,128)} %constant.12.clone.tw_ref, bf16[32,256]{1,0:T(8,128)(2,1)} %constant.18.second_ref), custom_call_target="tpu_custom_call" | custom-call | tf_op jit(solution)/shard_map/pallas_call | solution.py:213
  2.4 0.0 copy-start.2
  2.5 6.0 %all-to-all-start = ((bf16[8,32,128]{2,1,0:T(8,128)(2,1)}), bf16[8,32,128]{2,1,0:T(8,128)(2,1)S(1)}, u32[]{:S(2)}, u32[]{:S(2)}) async-start(bf16[8,32,128]{2,1,0:T(8,128)(2,1)} %bitcast.12), calls=%async_computation | async-start | bytes 131072 | tf_op jit(solution)/shard_map/all_to_all | solution.py:238
  8.4 0.0 copy-done.2
  8.4 27.2 %all_gather.3 = s32[256,256]{1,0:T(8,128)S(1)} all-gather(s32[16,256]{1,0:T(8,128)S(1)} %copy-done.2), channel_id=1, replica_groups=mesh['feed'=16,'chan'=8] {'feed'}, dimensions={0}, use_global_device_ids=true | all-gather | bytes 278528 | tf_op jit(solution)/shard_map/all_gather | solution.py:241
  35.6 0.0 copy-start.3
  35.6 0.7 copy-done.3
  36.3 0.6 reshape.30.owner_ref
  36.8 0.0 all-to-all-done
  36.8 0.0 copy-start.1
  36.8 0.6 copy-done.1
  37.5 1.7 %shard_map.74 = bf16[256,128]{1,0:T(8,128)(2,1)} custom-call(bf16[256,128]{1,0:T(8,128)(2,1)} %bitcast.14), custom_call_target="tpu_custom_call" | custom-call | tf_op jit(solution)/shard_map/pallas_call | solution.py:213
  39.1 3.4 %all-to-all-start.1 = ((bf16[16,16,128]{2,1,0:T(8,128)(2,1)}), bf16[16,16,128]{2,1,0:T(8,128)(2,1)S(1)}, u32[]{:S(2)}, u32[]{:S(2)}) async-start(bf16[16,16,128]{2,1,0:T(8,128)(2,1)} %bitcast.15), calls=%async_computation.1 | async-start | bytes 131072 | tf_op jit(solution)/shard_map/all_to_all | solution.py:240
  42.6 0.7 pad_add_fusion.code_ref
  43.2 6.7 %all-to-all-done.1 = bf16[16,16,128]{2,1,0:T(8,128)(2,1)S(1)} async-done(((bf16[16,16,128]{2,1,0:T(8,128)(2,1)}), bf16[16,16,128]{2,1,0:T(8,128)(2,1)S(1)}, u32[]{:S(2)}, u32[]{:S(2)}) %all-to-all-start.1) | async-done | bytes 65568 | tf_op jit(solution)/shard_map/all_to_all | solution.py:240
  50.0 0.0 copy-start
  50.0 0.6 copy-done
  50.6 10.7 %shard_map.75 = f32[16,16,128]{2,1,0:T(8,128)} custom-call(bf16[256,128]{1,0:T(8,128)(2,1)} %bitcast.13, s32[128,256]{1,0:T(8,128)} %pad_add_fusion.code_ref, s32[1,384]{1,0:T(1,128)} %reshape.30.owner_ref), custom_call_target="tpu_custom_call" | custom-call | tf_op jit(solution)/shard_map/pallas_call | solution.py:213
  61.3 12.1 %all_to_all.15 = f32[16,16,128]{2,1,0:T(8,128)} all-to-all(f32[16,16,128]{2,1,0:T(8,128)} %shard_map.75), channel_id=1, replica_groups=mesh['feed'=16,'chan'=8] {'feed'}, dimensions={0} | all-to-all | bytes 262144 | tf_op jit(solution)/shard_map/all_to_all | solution.py:255
  73.4 1.6 %shard_map.76 = f32[47,2,256]{2,1,0:T(2,128)} custom-call(f32[256,128]{1,0:T(8,128)} %bitcast.10), custom_call_target="tpu_custom_call" | custom-call | tf_op jit(solution)/shard_map/pallas_call | solution.py:213
  (2 shorter events, 0.0 us)
Async XLA Ops:
  2.4 6.0 %copy-start.2 = (s32[16,256]{1,0:T(8,128)S(1)}, s32[16,256]{1,0:T(8,128)}, u32[]{:S(2)}) copy-start(s32[16,256]{1,0:T(8,128)} %param.8) | copy-start | bytes 49156
  2.5 34.4 %all-to-all-start = ((bf16[8,32,128]{2,1,0:T(8,128)(2,1)}), bf16[8,32,128]{2,1,0:T(8,128)(2,1)S(1)}, u32[]{:S(2)}, u32[]{:S(2)}) async-start(bf16[8,32,128]{2,1,0:T(8,128)(2,1)} %bitcast.12), calls=%async_computation | async-start | bytes 131072 | tf_op jit(solution)/shard_map/all_to_all | solution.py:238
  35.6 0.7 copy-start.3
  36.8 0.6 copy-start.1
  39.1 10.8 %all-to-all-start.1 = ((bf16[16,16,128]{2,1,0:T(8,128)(2,1)}), bf16[16,16,128]{2,1,0:T(8,128)(2,1)S(1)}, u32[]{:S(2)}, u32[]{:S(2)}) async-start(bf16[16,16,128]{2,1,0:T(8,128)(2,1)} %bitcast.15), calls=%async_computation.1 | async-start | bytes 131072 | tf_op jit(solution)/shard_map/all_to_all | solution.py:240
  50.0 0.6 copy-start
where the time goes:
time: 75.6 us; the launch traced here: 75.1 us
  blocking collectives  39.3 us (52%)
  Pallas kernels  16.5 us (22%)
  starting transfers between devices  9.43 us (12%)
  waiting for transfers between devices  6.73 us (9%)
  local copies, waits for them, and re-layouts  2.5 us (3%)
    all_gather x1, blocking collectives, per_device(): codes = fold_codes(lax.all_gather(stack_code, 'feed', axis=0, tiled=True))  27.2 us
    pallas_call x4, Pallas kernels, call(): pl.pallas_call(kernel, out_shape=jax.ShapeDtypeStruct(shape, dtype), in_s...  16.5 us
    all_to_all x1, blocking collectives, per_device(): back = lax.all_to_all(msgs, 'feed', 0, 0, tiled=True)  12.1 us
    all_to_all x1, waiting for transfers between devices, per_device(): lax.all_to_all(regrouped.reshape(16, 16, 128), 'feed', 0, 0, tiled=True)  6.73 us
    all_to_all x1, starting transfers between devices, per_device(): got = lax.all_to_all(wide.reshape(8, 32, 128), 'chan', 0, 0, tiled=True)  5.98 us
    all_to_all x1, starting transfers between devices, per_device(): lax.all_to_all(regrouped.reshape(16, 16, 128), 'feed', 0, 0, tiled=True)  3.45 us
    unnamed x8, local copies, waits for them, and re-layouts  1.93 us
  transfers between devices with their start and end apart: 2, of which 1 were waited for; matrix products, arithmetic and copies ran while one was open for 2% of the time, Pallas kernels for 0%

commit v1 on v0

v1 whole, which is shorter than its diff:
```python
import math

import numpy as np
import jax
import jax.numpy as jnp
from jax import lax
from jax.experimental import pallas as pl
from jax.experimental.pallas import tpu as pltpu
from jax.sharding import PartitionSpec as P

SPECTRA = 4
TAPS = 8
FA = 64
FB = 128
FRAME = 8192
STACKS = 382
CAP = 47
FEEDS = 16
GROUPS = 8
INPUTS = 256
HALF = 128
CHUNK = 8
NB = 3
F32 = jnp.float32
BF16 = jnp.bfloat16
NT = (((1,), (1,)), ((), ()))


def window_table():
    length = TAPS * FRAME
    sample = np.arange(length, dtype=np.float64)
    centred = (sample - length / 2 + 0.5) / FRAME
    weights = np.sinc(centred) * (0.5 - 0.5 * np.cos(2.0 * np.pi * (sample + 0.5) / length))
    weights = weights * np.sqrt(FRAME / np.sum(weights * weights))
    return weights.reshape(TAPS, FA, FB).astype(np.float32)


def turns(left, right, modulus):
    return 2.0 * np.pi * (np.outer(left, right) % modulus) / modulus


def first_matrix():
    angles = turns(np.arange(FA), np.arange(FA), FA)
    parts = np.stack([np.cos(angles), -np.sin(angles)]).reshape(2, FA, 4, 16)
    out = np.zeros((2, 4, 2, 16, FA, 2), np.float32)
    for i in range(2):
        out[:, :, i, :, :, i] = parts.transpose(0, 2, 3, 1)
    return out.reshape(256, 128)


def twiddle_tables():
    angles = turns(np.arange(FA), np.arange(FB), FRAME).reshape(4, 1, 16, FB)
    angles = np.broadcast_to(angles, (4, 2, 16, FB)).reshape(128, FB)
    return np.stack([np.cos(angles), np.sin(angles)]).astype(np.float32)


def second_matrix():
    angles = turns(np.arange(32), np.arange(FB), FB)
    return np.concatenate([np.cos(angles), np.sin(angles)], axis=1).astype(np.float32)


def bf(table):
    return jnp.asarray(table).astype(BF16)


def channelize(x_ref, win_ref, first_ref, tw_ref, second_ref, mixed_ref, wide_ref):
    frames = []
    for t in range(SPECTRA):
        total = jnp.zeros((128, FB), F32)
        for p in range(TAPS):
            rows = x_ref[pl.ds((t + p) * 128, 128), :].astype(F32)
            total = total + win_ref[p] * rows
        frames.append(total.astype(BF16))
    frames = jnp.concatenate(frames, axis=1)
    section = jnp.dot(first_ref[...], frames, preferred_element_type=F32)
    cosine, sine = tw_ref[0], tw_ref[1]
    for t in range(SPECTRA):
        re = section[:128, t * FB : (t + 1) * FB]
        im = section[128:, t * FB : (t + 1) * FB]
        real = re * cosine + im * sine
        imag = im * cosine - re * sine
        minus = (-real).astype(BF16)
        real = real.astype(BF16)
        imag = imag.astype(BF16)
        for u in range(8):
            rows = slice(u * 16, u * 16 + 16)
            base = (u * 8 + t) * 16
            mixed_ref[base : base + 16, :FB] = real[rows]
            mixed_ref[base : base + 16, FB:] = imag[rows]
            base = (u * 8 + 4 + t) * 16
            mixed_ref[base : base + 16, :FB] = imag[rows]
            mixed_ref[base : base + 16, FB:] = minus[rows]
    out = lax.dot_general(second_ref[...], mixed_ref[...], NT, preferred_element_type=F32)
    out = out * (1.0 / math.sqrt(FRAME))
    for u in range(8):
        wide_ref[pl.ds(u, 32, stride=8), :] = out[:, u * 128 : (u + 1) * 128]
    return wide_ref[...].astype(BF16)


def regroup(block):
    row = lax.broadcasted_iota(jnp.int32, (256, 256), 0)
    col = lax.broadcasted_iota(jnp.int32, (256, 256), 1)
    source = ((row // 2) % 8) * 32 + (row // 16) * 2 + row % 2
    take = jnp.where(col == source, 1.0, 0.0).astype(BF16)
    return jnp.dot(take, block, preferred_element_type=F32).astype(BF16)


def prepare(code_ref, owner_ref, hi_ref, sign_ref, lo_ref, hot_ref, perm_ref, count_ref):
    codes = code_ref[...].reshape(INPUTS, INPUTS)
    row = lax.broadcasted_iota(jnp.int32, (HALF, HALF), 0)
    col = lax.broadcasted_iota(jnp.int32, (HALF, HALF), 1)
    low = jnp.where(col > row, codes[:HALF, :HALF], codes[HALF:, HALF:])
    code = jnp.concatenate([low, codes[:HALF, HALF:]], axis=1)
    row = lax.broadcasted_iota(jnp.int32, (HALF, INPUTS), 0)
    col = lax.broadcasted_iota(jnp.int32, (HALF, INPUTS), 1)
    target = jnp.where(code >= 0, code, -1 - code)
    sign_ref[...] = jnp.where(code >= 0, 1.0, -1.0).astype(F32)
    hi_ref[...] = lax.shift_right_logical(target, 7)
    lo_ref[...] = jnp.where(col != row, target & 127, -1)
    hot_row = lax.broadcasted_iota(jnp.int32, (128, INPUTS), 0)
    bid = lax.broadcasted_iota(jnp.int32, (16, INPUTS), 0)
    count_ref[...] = jnp.zeros_like(count_ref)

    @pl.loop(0, HALF // CHUNK)
    def _(step):
        marks = []
        hots = []
        for n in range(CHUNK):
            lo = lo_ref[pl.ds(step * CHUNK + n, 1), :]
            hi = hi_ref[pl.ds(step * CHUNK + n, 1), :]
            hots.append(jnp.where(hot_row == lo, 1.0, 0.0).astype(BF16))
            marks.append(jnp.where(hi == bid, 1.0, 0.0).astype(BF16))
        hot = jnp.concatenate(hots, axis=1)
        hot_ref[step] = hot
        mark = jnp.concatenate(marks, axis=1)
        count_ref[...] += lax.dot_general(mark, hot, NT, preferred_element_type=F32)

    owner = owner_ref[...]
    tall = jnp.transpose(jnp.broadcast_to(owner, (128, NB * 128)).astype(F32))
    cols = []
    for b in range(NB):
        mine = owner[:, b * 128 : (b + 1) * 128].astype(F32)
        row = lax.broadcasted_iota(jnp.int32, (NB * 128, 128), 0)
        col = lax.broadcasted_iota(jnp.int32, (NB * 128, 128), 1) + b * 128
        same = jnp.where((tall == mine) & (row < col), 1.0, 0.0)
        cols.append(jnp.sum(same, axis=0, keepdims=True))
    rank = jnp.concatenate(cols, axis=1).astype(jnp.int32)
    place = jnp.where(owner >= 0, owner * 128 + rank, -1)
    later = jnp.where(owner >= 0, place + 64, -1)
    both = jnp.concatenate([place, later], axis=1)
    slot = lax.broadcasted_iota(jnp.int32, (128, 2 * NB * 128), 0)
    for o in range(FEEDS):
        perm_ref[o] = jnp.where(slot + o * 128 == both, 1.0, 0.0).astype(BF16)


def stack_pairs(x_ref, hi_ref, sign_ref, hot_ref, xf_ref, left_ref, right_ref, data_ref, acc_ref):
    x = x_ref[...].reshape(INPUTS, 128)
    xf = x.astype(F32)
    xf_ref[0] = xf
    xf_ref[1] = jnp.concatenate([xf[:, 64:], -xf[:, :64]], axis=1)
    acc_ref[...] = jnp.zeros_like(acc_ref)
    lane = lax.broadcasted_iota(jnp.int32, (16, 128), 1)
    sub = lax.broadcasted_iota(jnp.int32, (16, 128), 0)
    pick = lane % 16 == sub
    lane_j = lax.broadcasted_iota(jnp.int32, (32, 128), 1)

    @pl.loop(0, HALF // CHUNK)
    def _(step):
        base = step * CHUNK
        for n in range(CHUNK):
            for q in range(2):
                at = slice(n * 32 + q * 16, n * 32 + q * 16 + 16)
                row = xf_ref[q, pl.ds(base + n, 1), :]
                left_ref[at, :] = jnp.where(pick, row, 0.0).astype(BF16)
                row = xf_ref[q, pl.ds(HALF + base + n, 1), :]
                right_ref[at, :] = jnp.where(pick, row, 0.0).astype(BF16)
        x = x_ref[...].reshape(INPUTS, 128)
        one = lax.dot_general(left_ref[...], x, NT, preferred_element_type=F32)
        two = lax.dot_general(right_ref[...], x[HALF:], NT, preferred_element_type=F32)
        for n in range(CHUNK):
            at = slice(n * 32, n * 32 + 32)
            low = jnp.where(lane_j > base + n, one[at, :128], two[at, :])
            both = jnp.concatenate([low, one[at, 128:]], axis=1)
            hi = hi_ref[pl.ds(base + n, 1), :]
            sign = sign_ref[pl.ds(base + n, 1), :]
            real = both[:16].astype(BF16)
            imag = (both[16:] * sign).astype(BF16)
            lanes = slice(n * INPUTS, (n + 1) * INPUTS)
            zero = jnp.zeros((), BF16)
            for b in range(NB):
                data_ref[b * 32 : b * 32 + 16, lanes] = jnp.where(hi == b, real, zero)
                data_ref[b * 32 + 16 : b * 32 + 32, lanes] = jnp.where(hi == b, imag, zero)
        acc_ref[...] += lax.dot_general(data_ref[...], hot_ref[step], NT, preferred_element_type=F32)


def messages(acc_ref, count_ref, perm_ref, send_ref):
    parts = []
    for q in range(2):
        for b in range(NB):
            sums = acc_ref[b * 32 + q * 16 : b * 32 + q * 16 + 16, :]
            parts.append(sums / jnp.maximum(count_ref[b : b + 1, :], 1.0))
    means = jnp.concatenate(parts, axis=1)
    high = means.astype(BF16)
    low = (means - high.astype(F32)).astype(BF16)
    both = jnp.concatenate([high, low], axis=0)
    perm = perm_ref[...].reshape(FEEDS * 128, 2 * NB * 128)
    out = lax.dot_general(both, perm, NT, preferred_element_type=F32)
    out = out[:16] + out[16:]
    for o in range(FEEDS):
        send_ref[o] = out[:, o * 128 : (o + 1) * 128]


def finish(block, out_ref):
    turned = jnp.transpose(block)
    out_ref[:, 0, :] = turned[:CAP]
    out_ref[:, 1, :] = turned[64 : 64 + CAP]


def exchange(buffer, target, send_sem, recv_sem, axis, size):
    me = lax.axis_index(axis)
    copies = []
    for d in range(1, size):
        peer = lax.rem(me + d, size)
        copies.append(
            pltpu.make_async_remote_copy(
                src_ref=buffer(peer),
                dst_ref=target.at[me],
                send_sem=send_sem.at[d],
                recv_sem=recv_sem.at[d],
                device_id={axis: peer},
                device_id_type=pl.DeviceIdType.MESH,
            )
        )
    for copy in copies:
        copy.start()

    def arrived():
        for d in range(1, size):
            source = lax.rem(me + size - d, size)
            pltpu.make_async_remote_copy(
                src_ref=buffer(source),
                dst_ref=target.at[source],
                send_sem=send_sem.at[d],
                recv_sem=recv_sem.at[d],
                device_id={axis: source},
                device_id_type=pl.DeviceIdType.MESH,
            ).wait_recv()

    def sent():
        for copy in copies:
            copy.wait_send()

    return arrived, sent


def kernel(
    x_hbm, win_hbm, first_hbm, tw_hbm, second_hbm, code_hbm, owner_hbm, out_ref,
    x_ref, win_ref, first_ref, tw_ref, second_ref, owner_ref,
    mixed_ref, wide_ref, wsend, wrecv, bsend, spec_ref, code_ref,
    hi_ref, sign_ref, lo_ref, hot_ref, perm_ref, count_ref,
    xf_ref, left_ref, right_ref, data_ref, acc_ref, msend, mrecv,
    local_sem, wss, wrs, css, crs, bss, brs, mss, mrs,
):
    feed = lax.axis_index("feed")
    chan = lax.axis_index("chan")
    loads = [
        pltpu.make_async_copy(a, b, local_sem.at[n])
        for n, (a, b) in enumerate([
            (x_hbm, x_ref), (win_hbm, win_ref), (first_hbm, first_ref), (tw_hbm, tw_ref),
            (second_hbm, second_ref), (code_hbm, code_ref.at[feed]), (owner_hbm, owner_ref),
        ])
    ]
    for load in loads:
        load.start()
    barrier = pltpu.get_barrier_semaphore()
    for d in range(1, GROUPS):
        pl.semaphore_signal(
            barrier, inc=1, device_id={"chan": lax.rem(chan + d, GROUPS)},
            device_id_type=pl.DeviceIdType.MESH,
        )
    for d in range(1, FEEDS):
        pl.semaphore_signal(
            barrier, inc=1, device_id={"feed": lax.rem(feed + d, FEEDS)},
            device_id_type=pl.DeviceIdType.MESH,
        )
    for load in loads:
        load.wait()
    wide = channelize(x_ref, win_ref, first_ref, tw_ref, second_ref, mixed_ref, wide_ref)
    wsend[...] = wide.reshape(GROUPS, 32, 128)
    pl.semaphore_wait(barrier, GROUPS + FEEDS - 2)
    w_arrived, w_sent = exchange(lambda d: wsend.at[d], wrecv, wss, wrs, "chan", GROUPS)
    c_arrived, c_sent = exchange(lambda d: code_ref.at[feed], code_ref, css, crs, "feed", FEEDS)
    wrecv[chan] = wsend[chan]
    w_arrived()
    bsend[...] = regroup(wrecv[...].reshape(256, 128)).reshape(FEEDS, 16, 128)
    b_arrived, b_sent = exchange(lambda d: bsend.at[d], spec_ref, bss, brs, "feed", FEEDS)
    spec_ref[feed] = bsend[feed]
    c_arrived()
    prepare(code_ref, owner_ref, hi_ref, sign_ref, lo_ref, hot_ref, perm_ref, count_ref)
    b_arrived()
    stack_pairs(spec_ref, hi_ref, sign_ref, hot_ref, xf_ref, left_ref, right_ref, data_ref, acc_ref)
    messages(acc_ref, count_ref, perm_ref, msend)
    m_arrived, m_sent = exchange(lambda d: msend.at[d], mrecv, mss, mrs, "feed", FEEDS)
    mrecv[feed] = msend[feed]
    m_arrived()
    finish(mrecv[...].reshape(256, 128), out_ref)
    w_sent()
    c_sent()
    b_sent()
    m_sent()


def per_device(raw_samples, stack_code, stack_owner):
    x = raw_samples.reshape(2, 704, 128).transpose(1, 0, 2).reshape(1408, 128)
    win = jnp.asarray(np.repeat(window_table(), 2, axis=1))
    owner = jnp.pad(stack_owner, (0, 2), constant_values=-1).reshape(1, NB * 128)
    rows = NB * 32
    dma = pltpu.SemaphoreType.DMA
    return pl.pallas_call(
        kernel,
        out_shape=jax.ShapeDtypeStruct((CAP, 2, 256), F32),
        in_specs=[pl.BlockSpec(memory_space=pl.ANY)] * 7,
        out_specs=pl.BlockSpec(memory_space=pltpu.VMEM),
        scratch_shapes=[
            pltpu.VMEM((1408, 128), BF16),
            pltpu.VMEM((TAPS, 128, 128), F32),
            pltpu.VMEM((256, 128), BF16),
            pltpu.VMEM((2, 128, 128), F32),
            pltpu.VMEM((32, 256), BF16),
            pltpu.VMEM((1, NB * 128), jnp.int32),
            pltpu.VMEM((1024, 256), BF16),
            pltpu.VMEM((256, 128), F32),
            pltpu.VMEM((GROUPS, 32, 128), BF16),
            pltpu.VMEM((GROUPS, 32, 128), BF16),
            pltpu.VMEM((FEEDS, 16, 128), BF16),
            pltpu.VMEM((FEEDS, 16, 128), BF16),
            pltpu.VMEM((FEEDS, 16, INPUTS), jnp.int32),
            pltpu.VMEM((HALF, INPUTS), jnp.int32),
            pltpu.VMEM((HALF, INPUTS), F32),
            pltpu.VMEM((HALF, INPUTS), jnp.int32),
            pltpu.VMEM((HALF // CHUNK, 128, CHUNK * INPUTS), BF16),
            pltpu.VMEM((FEEDS, 128, 2 * NB * 128), BF16),
            pltpu.VMEM((16, 128), F32),
            pltpu.VMEM((2, INPUTS, 128), F32),
            pltpu.VMEM((CHUNK * 32, 128), BF16),
            pltpu.VMEM((CHUNK * 32, 128), BF16),
            pltpu.VMEM((rows, CHUNK * INPUTS), BF16),
            pltpu.VMEM((rows, 128), F32),
            pltpu.VMEM((FEEDS, 16, 128), F32),
            pltpu.VMEM((FEEDS, 16, 128), F32),
            dma((7,)),
            dma((GROUPS,)), dma((GROUPS,)),
            dma((FEEDS,)), dma((FEEDS,)),
            dma((FEEDS,)), dma((FEEDS,)),
            dma((FEEDS,)), dma((FEEDS,)),
        ],
        compiler_params=pltpu.CompilerParams(
            vmem_limit_bytes=60 << 20, collective_id=0, has_side_effects=True
        ),
    )(x, win, bf(first_matrix()), jnp.asarray(twiddle_tables()), bf(second_matrix()), stack_code, owner)


def solution(mesh):
    placed = (P(("feed", "chan"), None), P("feed", None), P())
    return jax.shard_map(
        per_device, mesh=mesh, in_specs=placed, out_specs=P("feed", None, "chan"), check_vma=False
    )
```

time: 75.6 us -> 39.1 us (0.52)
  blocking collectives: 39.3 us -> 0 us
  Pallas kernels: 16.5 us -> 36.1 us
  starting transfers between devices: 9.43 us -> 0 us
  waiting for transfers between devices: 6.73 us -> 0 us
    all_gather x1 -> x0, blocking collectives: 27.2 us -> none  [per_device(): codes = fold_codes(lax.all_gather(stack_code, 'feed', axis=0, tiled=True))]
    pallas_call x4 -> x1, Pallas kernels: 16.5 us -> 36.1 us  [per_device(): pl.pallas_call(kernel, out_shape=jax.ShapeDtypeStruct((CAP, 2, 256), F32)...]
    all_to_all x1 -> x0, blocking collectives: 12.1 us -> none  [per_device(): back = lax.all_to_all(msgs, 'feed', 0, 0, tiled=True)]
    all_to_all x2 -> x0, starting transfers between devices: 9.43 us -> none  [the longest x1 5.98 us: per_device(): got = lax.all_to_all(wide.reshape(8, 32, 128), 'chan', 0, 0, tiled=True)]
    all_to_all x2 -> x0, waiting for transfers between devices: 6.73 us -> none  [the longest x1 6.73 us: per_device(): lax.all_to_all(regrouped.reshape(16, 16, 128), 'feed', 0, 0, tiled=True)]
    unnamed x8 -> x1, local copies, waits for them, and re-layouts: 1.93 us -> 1.54 us
  transfers between devices with their start and end apart: 2 -> 0, of which waited for: 1 -> 0; matrix products, arithmetic and copies ran while one was open for 2% -> 0% of each run, Pallas kernels for 0% -> 0%
where the time goes in v1:
time: 39.1 us; the launch traced here: 38.9 us
  Pallas kernels  36.1 us (92%)
  local copies, waits for them, and re-layouts  2.79 us (7%)
    pallas_call x1, Pallas kernels, per_device(): pl.pallas_call(kernel, out_shape=jax.ShapeDtypeStruct((CAP, 2, 256), F32)...  36.1 us
    unnamed x1, local copies, waits for them, and re-layouts  1.54 us

profile of v1, /device:TPU:1, one launch (start us, length us, event | category | flops | bytes accessed | tf_op | source)
XLA Modules:
  0.0 38.9 jit_solution(3106721777368486856)
XLA Ops:
  0.0 0.7 %pad.4 = s32[384]{0:T(512)S(1)} pad(s32[382]{0:T(512)} %param.9, s32[]{:T(128)} %constant.4.clone.1), padding=0_2 | pad | bytes 3068 | tf_op jit(solution)/shard_map/jit(_pad)/pad | solution.py:316
  0.7 0.6 %reshape.11.owner_hbm = s32[1,384]{1,0:T(1,128)} reshape(s32[384]{0:T(512)S(1)} %pad.4) | data formatting | bytes 3072 | tf_op jit(solution)/shard_map/reshape | solution.py:316
  1.3 36.1 %shard_map.73 = f32[47,2,256]{2,1,0:T(2,128)} custom-call(bf16[1408,128]{1,0:T(8,128)(2,1)} %bitcast.5, f32[8,128,128]{2,1,0:T(8,128)} %constant.10.clone.win_hbm, bf16[256,128]{1,0:T(8,128)(2,1)} %constant.17.first_hbm, f32[2,128,128]{2,1,0:T(8,128)} %constant.12.clone.tw_hbm, bf16[32,256]{1,0:T(8,128)(2,1)} %constant.18.second_hbm, s32[16,256]{1,0:T(8,128)} %code_hbm.1, ...), custom_call_target="tpu_custom_call" | custom-call | tf_op jit(solution)/shard_map/pallas_call | solution.py:319
  37.4 1.5 %copy.10 = f32[47,2,256]{2,1,0:T(2,128)} copy(f32[47,2,256]{2,1,0:T(2,128)} %shard_map.73) | data formatting | bytes 192512

commit v2 on v1

--- a/solution.py
+++ b/solution.py
@@ -105,36 +105,7 @@
     return jnp.dot(take, block, preferred_element_type=F32).astype(BF16)
 
 
-def prepare(code_ref, owner_ref, hi_ref, sign_ref, lo_ref, hot_ref, perm_ref, count_ref):
-    codes = code_ref[...].reshape(INPUTS, INPUTS)
-    row = lax.broadcasted_iota(jnp.int32, (HALF, HALF), 0)
-    col = lax.broadcasted_iota(jnp.int32, (HALF, HALF), 1)
-    low = jnp.where(col > row, codes[:HALF, :HALF], codes[HALF:, HALF:])
-    code = jnp.concatenate([low, codes[:HALF, HALF:]], axis=1)
-    row = lax.broadcasted_iota(jnp.int32, (HALF, INPUTS), 0)
-    col = lax.broadcasted_iota(jnp.int32, (HALF, INPUTS), 1)
-    target = jnp.where(code >= 0, code, -1 - code)
-    sign_ref[...] = jnp.where(code >= 0, 1.0, -1.0).astype(F32)
-    hi_ref[...] = lax.shift_right_logical(target, 7)
-    lo_ref[...] = jnp.where(col != row, target & 127, -1)
-    hot_row = lax.broadcasted_iota(jnp.int32, (128, INPUTS), 0)
-    bid = lax.broadcasted_iota(jnp.int32, (16, INPUTS), 0)
-    count_ref[...] = jnp.zeros_like(count_ref)
-
-    @pl.loop(0, HALF // CHUNK)
-    def _(step):
-        marks = []
-        hots = []
-        for n in range(CHUNK):
-            lo = lo_ref[pl.ds(step * CHUNK + n, 1), :]
-            hi = hi_ref[pl.ds(step * CHUNK + n, 1), :]
-            hots.append(jnp.where(hot_row == lo, 1.0, 0.0).astype(BF16))
-            marks.append(jnp.where(hi == bid, 1.0, 0.0).astype(BF16))
-        hot = jnp.concatenate(hots, axis=1)
-        hot_ref[step] = hot
-        mark = jnp.concatenate(marks, axis=1)
-        count_ref[...] += lax.dot_general(mark, hot, NT, preferred_element_type=F32)
-
+def permutation(owner_ref, perm_ref):
     owner = owner_ref[...]
     tall = jnp.transpose(jnp.broadcast_to(owner, (128, NB * 128)).astype(F32))
     cols = []
@@ -145,15 +116,51 @@
         same = jnp.where((tall == mine) & (row < col), 1.0, 0.0)
         cols.append(jnp.sum(same, axis=0, keepdims=True))
     rank = jnp.concatenate(cols, axis=1).astype(jnp.int32)
-    place = jnp.where(owner >= 0, owner * 128 + rank, -1)
-    later = jnp.where(owner >= 0, place + 64, -1)
-    both = jnp.concatenate([place, later], axis=1)
-    slot = lax.broadcasted_iota(jnp.int32, (128, 2 * NB * 128), 0)
-    for o in range(FEEDS):
-        perm_ref[o] = jnp.where(slot + o * 128 == both, 1.0, 0.0).astype(BF16)
-
-
-def stack_pairs(x_ref, hi_ref, sign_ref, hot_ref, xf_ref, left_ref, right_ref, data_ref, acc_ref):
+    place = jnp.where(owner >= 0, owner * 64 + rank, -1)
+
+    @pl.loop(0, FEEDS)
+    def _(o):
+        slot = lax.broadcasted_iota(jnp.int32, (64, NB * 128), 0) + o * 64
+        perm_ref[o] = jnp.where(slot == place, 1.0, 0.0).astype(BF16)
+
+
+def packed_row(ref, at):
+    return jnp.broadcast_to(ref[pl.ds(at, 1), :], (16, ref.shape[1])).astype(BF16)
+
+
+def prepare(code_ref, hi_ref, sign_ref, lo_ref, hot_ref, count_ref):
+    codes = code_ref[...].reshape(INPUTS, INPUTS).astype(jnp.int32)
+    row = lax.broadcasted_iota(jnp.int32, (HALF, HALF), 0)
+    col = lax.broadcasted_iota(jnp.int32, (HALF, HALF), 1)
+    low = jnp.where(col > row, codes[:HALF, :HALF], codes[HALF:, HALF:])
+    code = jnp.concatenate([low, codes[:HALF, HALF:]], axis=1)
+    row = lax.broadcasted_iota(jnp.int32, (HALF, INPUTS), 0)
+    col = lax.broadcasted_iota(jnp.int32, (HALF, INPUTS), 1)
+    target = jnp.where(code >= 0, code, -1 - code)
+    sign_ref[...] = jnp.where(code >= 0, 1.0, -1.0).astype(F32)
+    hi_ref[...] = lax.shift_right_logical(target, 7).astype(F32)
+    lo_ref[...] = jnp.where(col != row, target & 127, -1).astype(F32)
+    sub = lax.broadcasted_iota(jnp.int32, (16, INPUTS), 0)
+    rows = [(sub + r * 16).astype(F32).astype(BF16) for r in range(8)]
+    one, zero = jnp.ones((), BF16), jnp.zeros((), BF16)
+    count_ref[...] = jnp.zeros_like(count_ref)
+
+    @pl.loop(0, HALF // CHUNK)
+    def _(step):
+        marks = []
+        hots = []
+        for n in range(CHUNK):
+            lo = packed_row(lo_ref, step * CHUNK + n)
+            hi = packed_row(hi_ref, step * CHUNK + n)
+            hots.append(jnp.concatenate([jnp.where(lo == rows[r], one, zero) for r in range(8)], axis=0))
+            marks.append(jnp.where(hi == rows[0], one, zero))
+        hot = jnp.concatenate(hots, axis=1)
+        hot_ref[step] = hot
+        mark = jnp.concatenate(marks, axis=1)
+        count_ref[...] += lax.dot_general(mark, hot, NT, preferred_element_type=F32)
+
+
+def stack_pairs(x_ref, hi_ref, sign_ref, hot_ref, xf_ref, data_a, data_b, acc_ref):
     x = x_ref[...].reshape(INPUTS, 128)
     xf = x.astype(F32)
     xf_ref[0] = xf
@@ -161,59 +168,67 @@
     acc_ref[...] = jnp.zeros_like(acc_ref)
     lane = lax.broadcasted_iota(jnp.int32, (16, 128), 1)
     sub = lax.broadcasted_iota(jnp.int32, (16, 128), 0)
-    pick = lane % 16 == sub
+    pick = jnp.where(lane % 16 == sub, 1.0, 0.0).astype(BF16)
     lane_j = lax.broadcasted_iota(jnp.int32, (32, 128), 1)
-
-    @pl.loop(0, HALF // CHUNK)
-    def _(step):
+    zero = jnp.zeros((), BF16)
+
+    def produce(step, data_ref):
         base = step * CHUNK
+        left, right = [], []
         for n in range(CHUNK):
             for q in range(2):
-                at = slice(n * 32 + q * 16, n * 32 + q * 16 + 16)
-                row = xf_ref[q, pl.ds(base + n, 1), :]
-                left_ref[at, :] = jnp.where(pick, row, 0.0).astype(BF16)
-                row = xf_ref[q, pl.ds(HALF + base + n, 1), :]
-                right_ref[at, :] = jnp.where(pick, row, 0.0).astype(BF16)
+                left.append(packed_row(xf_ref.at[q], base + n) * pick)
+                right.append(packed_row(xf_ref.at[q], HALF + base + n) * pick)
+        left = jnp.concatenate(left, axis=0)
+        right = jnp.concatenate(right, axis=0)
         x = x_ref[...].reshape(INPUTS, 128)
-        one = lax.dot_general(left_ref[...], x, NT, preferred_element_type=F32)
-        two = lax.dot_general(right_ref[...], x[HALF:], NT, preferred_element_type=F32)
+        one = lax.dot_general(left, x, NT, preferred_element_type=F32)
+        two = lax.dot_general(right, x[HALF:], NT, preferred_element_type=F32)
         for n in range(CHUNK):
             at = slice(n * 32, n * 32 + 32)
             low = jnp.where(lane_j > base + n, one[at, :128], two[at, :])
-            both = jnp.concatenate([low, one[at, 128:]], axis=1)
-            hi = hi_ref[pl.ds(base + n, 1), :]
-            sign = sign_ref[pl.ds(base + n, 1), :]
-            real = both[:16].astype(BF16)
-            imag = (both[16:] * sign).astype(BF16)
+            both = jnp.concatenate([low, one[at, 128:]], axis=1).astype(BF16)
+            hi = packed_row(hi_ref, base + n)
+            sign = packed_row(sign_ref, base + n)
+            real = both[:16]
+            imag = both[16:] * sign
             lanes = slice(n * INPUTS, (n + 1) * INPUTS)
-            zero = jnp.zeros((), BF16)
             for b in range(NB):
-                data_ref[b * 32 : b * 32 + 16, lanes] = jnp.where(hi == b, real, zero)
-                data_ref[b * 32 + 16 : b * 32 + 32, lanes] = jnp.where(hi == b, imag, zero)
+                mine = hi == jnp.full((16, INPUTS), b, BF16)
+                data_ref[b * 32 : b * 32 + 16, lanes] = jnp.where(mine, real, zero)
+                data_ref[b * 32 + 16 : b * 32 + 32, lanes] = jnp.where(mine, imag, zero)
+
+    def consume(step, data_ref):
         acc_ref[...] += lax.dot_general(data_ref[...], hot_ref[step], NT, preferred_element_type=F32)
+
+    steps = HALF // CHUNK
+    produce(0, data_a)
+
+    @pl.loop(0, steps // 2)
+    def _(k):
+        produce(2 * k + 1, data_b)
+        consume(2 * k, data_a)
+        produce(jnp.minimum(2 * k + 2, steps - 1), data_a)
+        consume(2 * k + 1, data_b)
 
 
 def messages(acc_ref, count_ref, perm_ref, send_ref):
     parts = []
-    for q in range(2):
-        for b in range(NB):
-            sums = acc_ref[b * 32 + q * 16 : b * 32 + q * 16 + 16, :]
-            parts.append(sums / jnp.maximum(count_ref[b : b + 1, :], 1.0))
-    means = jnp.concatenate(parts, axis=1)
-    high = means.astype(BF16)
-    low = (means - high.astype(F32)).astype(BF16)
-    both = jnp.concatenate([high, low], axis=0)
-    perm = perm_ref[...].reshape(FEEDS * 128, 2 * NB * 128)
-    out = lax.dot_general(both, perm, NT, preferred_element_type=F32)
-    out = out[:16] + out[16:]
-    for o in range(FEEDS):
-        send_ref[o] = out[:, o * 128 : (o + 1) * 128]
+    for b in range(NB):
+        parts.append(acc_ref[b * 32 : b * 32 + 32, :] / jnp.maximum(count_ref[b : b + 1, :], 1.0))
+    means = jnp.concatenate(parts, axis=1).astype(BF16)
+    perm = perm_ref[...].reshape(FEEDS * 64, NB * 128)
+    out = lax.dot_general(means, perm, NT, preferred_element_type=F32)
+    first = lax.broadcasted_iota(jnp.int32, (16, 128), 1) < 64
+    for o in range(0, FEEDS, 2):
+        real = out[:16, o * 64 : o * 64 + 128]
+        imag = out[16:, o * 64 : o * 64 + 128]
+        send_ref[o] = jnp.where(first, real, pltpu.roll(imag, 64, 1)).astype(BF16)
+        send_ref[o + 1] = jnp.where(first, pltpu.roll(real, 64, 1), imag).astype(BF16)
 
 
 def finish(block, out_ref):
-    turned = jnp.transpose(block)
-    out_ref[:, 0, :] = turned[:CAP]
-    out_ref[:, 1, :] = turned[64 : 64 + CAP]
+    out_ref[...] = jnp.transpose(block.astype(F32))
 
 
 def exchange(buffer, target, send_sem, recv_sem, axis, size):
@@ -255,10 +270,10 @@
 
 def kernel(
     x_hbm, win_hbm, first_hbm, tw_hbm, second_hbm, code_hbm, owner_hbm, out_ref,
-    x_ref, win_ref, first_ref, tw_ref, second_ref, owner_ref,
+    x_ref, win_ref, first_ref, tw_ref, second_ref, owner_ref, raw_code,
     mixed_ref, wide_ref, wsend, wrecv, bsend, spec_ref, code_ref,
     hi_ref, sign_ref, lo_ref, hot_ref, perm_ref, count_ref,
-    xf_ref, left_ref, right_ref, data_ref, acc_ref, msend, mrecv,
+    xf_ref, data_a, data_b, acc_ref, msend, mrecv,
     local_sem, wss, wrs, css, crs, bss, brs, mss, mrs,
 ):
     feed = lax.axis_index("feed")
@@ -267,7 +282,7 @@
         pltpu.make_async_copy(a, b, local_sem.at[n])
         for n, (a, b) in enumerate([
             (x_hbm, x_ref), (win_hbm, win_ref), (first_hbm, first_ref), (tw_hbm, tw_ref),
-            (second_hbm, second_ref), (code_hbm, code_ref.at[feed]), (owner_hbm, owner_ref),
+            (second_hbm, second_ref), (code_hbm, raw_code), (owner_hbm, owner_ref),
         ])
     ]
     for load in loads:
@@ -287,6 +302,8 @@
         load.wait()
     wide = channelize(x_ref, win_ref, first_ref, tw_ref, second_ref, mixed_ref, wide_ref)
     wsend[...] = wide.reshape(GROUPS, 32, 128)
+    code_ref[feed] = raw_code[...].astype(jnp.int16)
+    permutation(owner_ref, perm_ref)
     pl.semaphore_wait(barrier, GROUPS + FEEDS - 2)
     w_arrived, w_sent = exchange(lambda d: wsend.at[d], wrecv, wss, wrs, "chan", GROUPS)
     c_arrived, c_sent = exchange(lambda d: code_ref.at[feed], code_ref, css, crs, "feed", FEEDS)
@@ -296,9 +313,9 @@
     b_arrived, b_sent = exchange(lambda d: bsend.at[d], spec_ref, bss, brs, "feed", FEEDS)
     spec_ref[feed] = bsend[feed]
     c_arrived()
-    prepare(code_ref, owner_ref, hi_ref, sign_ref, lo_ref, hot_ref, perm_ref, count_ref)
+    prepare(code_ref, hi_ref, sign_ref, lo_ref, hot_ref, count_ref)
     b_arrived()
-    stack_pairs(spec_ref, hi_ref, sign_ref, hot_ref, xf_ref, left_ref, right_ref, data_ref, acc_ref)
+    stack_pairs(spec_ref, hi_ref, sign_ref, hot_ref, xf_ref, data_a, data_b, acc_ref)
     messages(acc_ref, count_ref, perm_ref, msend)
     m_arrived, m_sent = exchange(lambda d: msend.at[d], mrecv, mss, mrs, "feed", FEEDS)
     mrecv[feed] = msend[feed]
@@ -316,9 +333,9 @@
     owner = jnp.pad(stack_owner, (0, 2), constant_values=-1).reshape(1, NB * 128)
     rows = NB * 32
     dma = pltpu.SemaphoreType.DMA
-    return pl.pallas_call(
+    turned = pl.pallas_call(
         kernel,
-        out_shape=jax.ShapeDtypeStruct((CAP, 2, 256), F32),
+        out_shape=jax.ShapeDtypeStruct((128, 256), F32),
         in_specs=[pl.BlockSpec(memory_space=pl.ANY)] * 7,
         out_specs=pl.BlockSpec(memory_space=pltpu.VMEM),
         scratch_shapes=[
@@ -328,26 +345,26 @@
             pltpu.VMEM((2, 128, 128), F32),
             pltpu.VMEM((32, 256), BF16),
             pltpu.VMEM((1, NB * 128), jnp.int32),
+            pltpu.VMEM((16, INPUTS), jnp.int32),
             pltpu.VMEM((1024, 256), BF16),
             pltpu.VMEM((256, 128), F32),
             pltpu.VMEM((GROUPS, 32, 128), BF16),
             pltpu.VMEM((GROUPS, 32, 128), BF16),
             pltpu.VMEM((FEEDS, 16, 128), BF16),
             pltpu.VMEM((FEEDS, 16, 128), BF16),
-            pltpu.VMEM((FEEDS, 16, INPUTS), jnp.int32),
-            pltpu.VMEM((HALF, INPUTS), jnp.int32),
+            pltpu.VMEM((FEEDS, 16, INPUTS), jnp.int16),
             pltpu.VMEM((HALF, INPUTS), F32),
-            pltpu.VMEM((HALF, INPUTS), jnp.int32),
+            pltpu.VMEM((HALF, INPUTS), F32),
+            pltpu.VMEM((HALF, INPUTS), F32),
             pltpu.VMEM((HALF // CHUNK, 128, CHUNK * INPUTS), BF16),
-            pltpu.VMEM((FEEDS, 128, 2 * NB * 128), BF16),
+            pltpu.VMEM((FEEDS, 64, NB * 128), BF16),
             pltpu.VMEM((16, 128), F32),
             pltpu.VMEM((2, INPUTS, 128), F32),
-            pltpu.VMEM((CHUNK * 32, 128), BF16),
-            pltpu.VMEM((CHUNK * 32, 128), BF16),
+            pltpu.VMEM((rows, CHUNK * INPUTS), BF16),
             pltpu.VMEM((rows, CHUNK * INPUTS), BF16),
             pltpu.VMEM((rows, 128), F32),
-            pltpu.VMEM((FEEDS, 16, 128), F32),
-            pltpu.VMEM((FEEDS, 16, 128), F32),
+            pltpu.VMEM((FEEDS, 16, 128), BF16),
+            pltpu.VMEM((FEEDS, 16, 128), BF16),
             dma((7,)),
             dma((GROUPS,)), dma((GROUPS,)),
             dma((FEEDS,)), dma((FEEDS,)),
@@ -358,6 +375,7 @@
             vmem_limit_bytes=60 << 20, collective_id=0, has_side_effects=True
         ),
     )(x, win, bf(first_matrix()), jnp.asarray(twiddle_tables()), bf(second_matrix()), stack_code, owner)
+    return turned.reshape(2, 64, 256)[:, :CAP].transpose(1, 0, 2)
 
 
 def solution(mesh):

time: 39.1 us -> 32.6 us (0.83)
  Pallas kernels: 36.1 us -> 29.5 us
    pallas_call x1, Pallas kernels: 36.1 us -> 29.5 us  [per_device(): pl.pallas_call(kernel, out_shape=jax.ShapeDtypeStruct((128, 256), F32), i...]
    slice x0 -> x1, local copies, waits for them, and re-layouts: none -> 0.9 us  [per_device(): return turned.reshape(2, 64, 256)[:, :CAP].transpose(1, 0, 2)]
    unnamed x1, local copies, waits for them, and re-layouts: 1.54 us -> 0.71 us
where the time goes in v2:
time: 32.6 us; the launch traced here: 32.4 us
  Pallas kernels  29.5 us (90%)
  local copies, waits for them, and re-layouts  2.87 us (9%)
    pallas_call x1, Pallas kernels, per_device(): pl.pallas_call(kernel, out_shape=jax.ShapeDtypeStruct((128, 256), F32), i...  29.5 us
    slice x1, local copies, waits for them, and re-layouts, per_device(): return turned.reshape(2, 64, 256)[:, :CAP].transpose(1, 0, 2)  0.9 us
    unnamed x1, local copies, waits for them, and re-layouts  0.71 us
    pad x1, local copies, waits for them, and re-layouts, per_device(): jnp.pad(stack_owner, (0, 2), constant_values=-1).reshape(1, NB * 128)  0.68 us

profile of v2, /device:TPU:1, one launch (start us, length us, event | category | flops | bytes accessed | tf_op | source)
XLA Modules:
  0.0 32.4 jit_solution(3850773458272819808)
XLA Ops:
  0.0 0.7 %pad.4 = s32[384]{0:T(512)S(1)} pad(s32[382]{0:T(512)} %param.9, s32[]{:T(128)} %constant.4.clone.1), padding=0_2 | pad | bytes 3068 | tf_op jit(solution)/shard_map/jit(_pad)/pad | solution.py:333
  0.7 0.6 %reshape.14.owner_hbm = s32[1,384]{1,0:T(1,128)} reshape(s32[384]{0:T(512)S(1)} %pad.4) | data formatting | bytes 3072 | tf_op jit(solution)/shard_map/reshape | solution.py:333
  1.3 29.5 %shard_map.73 = f32[128,256]{1,0:T(8,128)} custom-call(bf16[1408,128]{1,0:T(8,128)(2,1)} %bitcast.10, f32[8,128,128]{2,1,0:T(8,128)} %constant.10.clone.win_hbm, bf16[256,128]{1,0:T(8,128)(2,1)} %constant.17.first_hbm, f32[2,128,128]{2,1,0:T(8,128)} %constant.12.clone.tw_hbm, bf16[32,256]{1,0:T(8,128)(2,1)} %constant.18.second_hbm, s32[16,256]{1,0:T(8,128)} %code_hbm.1, ...), custom_call_target="tpu_custom_call" | custom-call | tf_op jit(solution)/shard_map/pallas_call | solution.py:336
  30.8 0.9 %slice.4 = f32[2,47,256]{2,1,0:T(8,128)S(1)} slice(f32[2,64,256]{2,1,0:T(8,128)} %bitcast.9), slice={[0:2], [0:47], [0:256]} | slice | bytes 192512 | tf_op jit(solution)/shard_map/slice | solution.py:378
  31.7 0.7 %copy.12 = f32[2,47,256]{2,0,1:T(2,128)} copy(f32[2,47,256]{2,1,0:T(8,128)S(1)} %slice.4) | data formatting | bytes 192512

commit v3 on v2

--- a/solution.py
+++ b/solution.py
@@ -106,7 +106,7 @@
 
 
 def permutation(owner_ref, perm_ref):
-    owner = owner_ref[...]
+    owner = jnp.concatenate([owner_ref[...].reshape(1, STACKS), jnp.full((1, NB * 128 - STACKS), -1, jnp.int32)], axis=1)
     tall = jnp.transpose(jnp.broadcast_to(owner, (128, NB * 128)).astype(F32))
     cols = []
     for b in range(NB):
@@ -152,10 +152,12 @@
         for n in range(CHUNK):
             lo = packed_row(lo_ref, step * CHUNK + n)
             hi = packed_row(hi_ref, step * CHUNK + n)
-            hots.append(jnp.concatenate([jnp.where(lo == rows[r], one, zero) for r in range(8)], axis=0))
+            hot = jnp.concatenate([jnp.where(lo == rows[r], one, zero) for r in range(8)], axis=0)
+            hot_ref[step, 2 * n] = hot[:, :128]
+            hot_ref[step, 2 * n + 1] = hot[:, 128:]
+            hots.append(hot)
             marks.append(jnp.where(hi == rows[0], one, zero))
         hot = jnp.concatenate(hots, axis=1)
-        hot_ref[step] = hot
         mark = jnp.concatenate(marks, axis=1)
         count_ref[...] += lax.dot_general(mark, hot, NT, preferred_element_type=F32)
 
@@ -192,14 +194,19 @@
             sign = packed_row(sign_ref, base + n)
             real = both[:16]
             imag = both[16:] * sign
-            lanes = slice(n * INPUTS, (n + 1) * INPUTS)
             for b in range(NB):
                 mine = hi == jnp.full((16, INPUTS), b, BF16)
-                data_ref[b * 32 : b * 32 + 16, lanes] = jnp.where(mine, real, zero)
-                data_ref[b * 32 + 16 : b * 32 + 32, lanes] = jnp.where(mine, imag, zero)
+                re = jnp.where(mine, real, zero)
+                im = jnp.where(mine, imag, zero)
+                for h in range(2):
+                    half = slice(h * 128, h * 128 + 128)
+                    data_ref[2 * n + h, b * 32 : b * 32 + 16, :] = re[:, half]
+                    data_ref[2 * n + h, b * 32 + 16 : b * 32 + 32, :] = im[:, half]
 
     def consume(step, data_ref):
-        acc_ref[...] += lax.dot_general(data_ref[...], hot_ref[step], NT, preferred_element_type=F32)
+        data = jnp.concatenate([data_ref[m] for m in range(2 * CHUNK)], axis=1)
+        hot = jnp.concatenate([hot_ref[step, m] for m in range(2 * CHUNK)], axis=1)
+        acc_ref[...] += lax.dot_general(data, hot, NT, preferred_element_type=F32)
 
     steps = HALF // CHUNK
     produce(0, data_a)
@@ -228,44 +235,60 @@
 
 
 def finish(block, out_ref):
-    out_ref[...] = jnp.transpose(block.astype(F32))
-
-
-def exchange(buffer, target, send_sem, recv_sem, axis, size):
+    turned = jnp.transpose(block.astype(F32))
+    for h in range(2):
+        for q in range(2):
+            out_ref[pl.ds(2 * h + q, CAP, stride=4), :] = turned[q * 64 : q * 64 + CAP, h * 128 : h * 128 + 128]
+
+
+def far_first(axis):
+    if axis == "feed":
+        sizes, weights = (4, 2, 2), ((0, 3, 6, 3), (0, 6), (0, 1))
+    else:
+        sizes, weights = (4, 2), ((0, 3, 6, 3), (0, 3))
+    offsets = [o for o in np.ndindex(*sizes) if any(o)]
+    offsets.sort(key=lambda o: -sum(w[n] for w, n in zip(weights, o)))
+    return sizes, offsets
+
+
+def peers(axis):
     me = lax.axis_index(axis)
-    copies = []
-    for d in range(1, size):
-        peer = lax.rem(me + d, size)
-        copies.append(
-            pltpu.make_async_remote_copy(
-                src_ref=buffer(peer),
-                dst_ref=target.at[me],
-                send_sem=send_sem.at[d],
-                recv_sem=recv_sem.at[d],
-                device_id={axis: peer},
-                device_id_type=pl.DeviceIdType.MESH,
-            )
-        )
-    for copy in copies:
-        copy.start()
-
-    def arrived():
-        for d in range(1, size):
-            source = lax.rem(me + size - d, size)
-            pltpu.make_async_remote_copy(
-                src_ref=buffer(source),
-                dst_ref=target.at[source],
-                send_sem=send_sem.at[d],
-                recv_sem=recv_sem.at[d],
-                device_id={axis: source},
-                device_id_type=pl.DeviceIdType.MESH,
-            ).wait_recv()
-
-    def sent():
-        for copy in copies:
-            copy.wait_send()
-
-    return arrived, sent
+    sizes, offsets = far_first(axis)
+    place, rest = [], me
+    for size in reversed(sizes):
+        place.insert(0, lax.rem(rest, size))
+        rest = rest // size
+    out = []
+    for offset in offsets:
+        peer = 0
+        for size, at, step in zip(sizes, place, offset):
+            peer = peer * size + lax.rem(at + step, size)
+        out.append(peer)
+    return out
+
+
+def exchange(buffer, target, send_sem, recv_sem, axis):
+    me = lax.axis_index(axis)
+    others = peers(axis)
+    for peer in others:
+        pltpu.make_async_remote_copy(
+            src_ref=buffer(peer),
+            dst_ref=target.at[me],
+            send_sem=send_sem,
+            recv_sem=recv_sem,
+            device_id={axis: peer},
+            device_id_type=pl.DeviceIdType.MESH,
+        ).start()
+    whole = target.at[pl.ds(0, len(others))]
+    every = pltpu.make_async_remote_copy(
+        src_ref=whole,
+        dst_ref=whole,
+        send_sem=send_sem,
+        recv_sem=recv_sem,
+        device_id={axis: others[0]},
+        device_id_type=pl.DeviceIdType.MESH,
+    )
+    return every.wait_recv, every.wait_send
 
 
 def kernel(
@@ -278,6 +301,12 @@
 ):
     feed = lax.axis_index("feed")
     chan = lax.axis_index("chan")
+    barrier = pltpu.get_barrier_semaphore()
+    for axis in ("chan", "feed"):
+        for peer in peers(axis):
+            pl.semaphore_signal(
+                barrier, inc=1, device_id={axis: peer}, device_id_type=pl.DeviceIdType.MESH
+            )
     loads = [
         pltpu.make_async_copy(a, b, local_sem.at[n])
         for n, (a, b) in enumerate([
@@ -287,17 +316,6 @@
     ]
     for load in loads:
         load.start()
-    barrier = pltpu.get_barrier_semaphore()
-    for d in range(1, GROUPS):
-        pl.semaphore_signal(
-            barrier, inc=1, device_id={"chan": lax.rem(chan + d, GROUPS)},
-            device_id_type=pl.DeviceIdType.MESH,
-        )
-    for d in range(1, FEEDS):
-        pl.semaphore_signal(
-            barrier, inc=1, device_id={"feed": lax.rem(feed + d, FEEDS)},
-            device_id_type=pl.DeviceIdType.MESH,
-        )
     for load in loads:
         load.wait()
     wide = channelize(x_ref, win_ref, first_ref, tw_ref, second_ref, mixed_ref, wide_ref)
@@ -305,19 +323,19 @@
     code_ref[feed] = raw_code[...].astype(jnp.int16)
     permutation(owner_ref, perm_ref)
     pl.semaphore_wait(barrier, GROUPS + FEEDS - 2)
-    w_arrived, w_sent = exchange(lambda d: wsend.at[d], wrecv, wss, wrs, "chan", GROUPS)
-    c_arrived, c_sent = exchange(lambda d: code_ref.at[feed], code_ref, css, crs, "feed", FEEDS)
+    w_arrived, w_sent = exchange(lambda d: wsend.at[d], wrecv, wss, wrs, "chan")
+    c_arrived, c_sent = exchange(lambda d: code_ref.at[feed], code_ref, css, crs, "feed")
     wrecv[chan] = wsend[chan]
     w_arrived()
     bsend[...] = regroup(wrecv[...].reshape(256, 128)).reshape(FEEDS, 16, 128)
-    b_arrived, b_sent = exchange(lambda d: bsend.at[d], spec_ref, bss, brs, "feed", FEEDS)
+    b_arrived, b_sent = exchange(lambda d: bsend.at[d], spec_ref, bss, brs, "feed")
     spec_ref[feed] = bsend[feed]
     c_arrived()
     prepare(code_ref, hi_ref, sign_ref, lo_ref, hot_ref, count_ref)
     b_arrived()
     stack_pairs(spec_ref, hi_ref, sign_ref, hot_ref, xf_ref, data_a, data_b, acc_ref)
     messages(acc_ref, count_ref, perm_ref, msend)
-    m_arrived, m_sent = exchange(lambda d: msend.at[d], mrecv, mss, mrs, "feed", FEEDS)
+    m_arrived, m_sent = exchange(lambda d: msend.at[d], mrecv, mss, mrs, "feed")
     mrecv[feed] = msend[feed]
     m_arrived()
     finish(mrecv[...].reshape(256, 128), out_ref)
@@ -330,12 +348,12 @@
 def per_device(raw_samples, stack_code, stack_owner):
     x = raw_samples.reshape(2, 704, 128).transpose(1, 0, 2).reshape(1408, 128)
     win = jnp.asarray(np.repeat(window_table(), 2, axis=1))
-    owner = jnp.pad(stack_owner, (0, 2), constant_values=-1).reshape(1, NB * 128)
+    owner = stack_owner
     rows = NB * 32
     dma = pltpu.SemaphoreType.DMA
     turned = pl.pallas_call(
         kernel,
-        out_shape=jax.ShapeDtypeStruct((128, 256), F32),
+        out_shape=jax.ShapeDtypeStruct((4 * CAP, 128), F32),
         in_specs=[pl.BlockSpec(memory_space=pl.ANY)] * 7,
         out_specs=pl.BlockSpec(memory_space=pltpu.VMEM),
         scratch_shapes=[
@@ -344,7 +362,7 @@
             pltpu.VMEM((256, 128), BF16),
             pltpu.VMEM((2, 128, 128), F32),
             pltpu.VMEM((32, 256), BF16),
-            pltpu.VMEM((1, NB * 128), jnp.int32),
+            pltpu.VMEM((STACKS,), jnp.int32),
             pltpu.VMEM((16, INPUTS), jnp.int32),
             pltpu.VMEM((1024, 256), BF16),
             pltpu.VMEM((256, 128), F32),
@@ -356,26 +374,23 @@
             pltpu.VMEM((HALF, INPUTS), F32),
             pltpu.VMEM((HALF, INPUTS), F32),
             pltpu.VMEM((HALF, INPUTS), F32),
-            pltpu.VMEM((HALF // CHUNK, 128, CHUNK * INPUTS), BF16),
+            pltpu.VMEM((HALF // CHUNK, 2 * CHUNK, 128, 128), BF16),
             pltpu.VMEM((FEEDS, 64, NB * 128), BF16),
             pltpu.VMEM((16, 128), F32),
             pltpu.VMEM((2, INPUTS, 128), F32),
-            pltpu.VMEM((rows, CHUNK * INPUTS), BF16),
-            pltpu.VMEM((rows, CHUNK * INPUTS), BF16),
+            pltpu.VMEM((2 * CHUNK, rows, 128), BF16),
+            pltpu.VMEM((2 * CHUNK, rows, 128), BF16),
             pltpu.VMEM((rows, 128), F32),
             pltpu.VMEM((FEEDS, 16, 128), BF16),
             pltpu.VMEM((FEEDS, 16, 128), BF16),
             dma((7,)),
-            dma((GROUPS,)), dma((GROUPS,)),
-            dma((FEEDS,)), dma((FEEDS,)),
-            dma((FEEDS,)), dma((FEEDS,)),
-            dma((FEEDS,)), dma((FEEDS,)),
+            dma, dma, dma, dma, dma, dma, dma, dma,
         ],
         compiler_params=pltpu.CompilerParams(
             vmem_limit_bytes=60 << 20, collective_id=0, has_side_effects=True
         ),
     )(x, win, bf(first_matrix()), jnp.asarray(twiddle_tables()), bf(second_matrix()), stack_code, owner)
-    return turned.reshape(2, 64, 256)[:, :CAP].transpose(1, 0, 2)
+    return turned.reshape(CAP, 2, 2, 128).transpose(0, 2, 1, 3).reshape(CAP, 2, 256)
 
 
 def solution(mesh):

time: 32.6 us -> 30 us (0.920)
  local copies, waits for them, and re-layouts: 2.87 us -> 1.59 us
  Pallas kernels: 29.5 us -> 28.3 us
    pallas_call x1, Pallas kernels: 29.5 us -> 28.3 us  [per_device(): pl.pallas_call(kernel, out_shape=jax.ShapeDtypeStruct((4 * CAP, 128), F32...]
    reshape x1, local copies, waits for them, and re-layouts: 0.57 us -> 1.59 us  [per_device(): turned.reshape(CAP, 2, 2, 128).transpose(0, 2, 1, 3).reshape(CAP, 2, 256)]
    slice x1 -> x0, local copies, waits for them, and re-layouts: 0.9 us -> none  [per_device(): return turned.reshape(2, 64, 256)[:, :CAP].transpose(1, 0, 2)]
    unnamed x1 -> x0, local copies, waits for them, and re-layouts: 0.71 us -> none
    pad x1 -> x0, local copies, waits for them, and re-layouts: 0.68 us -> none  [per_device(): jnp.pad(stack_owner, (0, 2), constant_values=-1).reshape(1, NB * 128)]
where the time goes in v3:
time: 30 us; the launch traced here: 29.9 us
  Pallas kernels  28.3 us (94%)
  local copies, waits for them, and re-layouts  1.59 us (5%)
    pallas_call x1, Pallas kernels, per_device(): pl.pallas_call(kernel, out_shape=jax.ShapeDtypeStruct((4 * CAP, 128), F32...  28.3 us
    reshape x1, local copies, waits for them, and re-layouts, per_device(): turned.reshape(CAP, 2, 2, 128).transpose(0, 2, 1, 3).reshape(CAP, 2, 256)  1.59 us

profile of v3, /device:TPU:1, one launch (start us, length us, event | category | flops | bytes accessed | tf_op | source)
XLA Modules:
  0.0 29.9 jit_solution(2220008417290600618)
XLA Ops:
  0.0 28.3 %shard_map.73 = f32[188,128]{1,0:T(8,128)} custom-call(bf16[1408,128]{1,0:T(8,128)(2,1)} %bitcast.8, f32[8,128,128]{2,1,0:T(8,128)} %constant.8.clone.win_hbm, bf16[256,128]{1,0:T(8,128)(2,1)} %constant.13.first_hbm, f32[2,128,128]{2,1,0:T(8,128)} %constant.10.clone.tw_hbm, bf16[32,256]{1,0:T(8,128)(2,1)} %constant.14.second_hbm, s32[16,256]{1,0:T(8,128)} %code_hbm.1, ...), custom_call_target="tpu_custom_call" | custom-call | tf_op jit(solution)/shard_map/pallas_call | solution.py:354
  28.3 1.6 %reshape.14 = f32[47,2,2,128]{3,2,1,0:T(2,128)} reshape(f32[188,128]{1,0:T(8,128)} %shard_map.73) | data formatting | bytes 192512 | tf_op jit(solution)/shard_map/reshape | solution.py:393

commit v4 on v3

--- a/solution.py
+++ b/solution.py
@@ -20,6 +20,8 @@
 INPUTS = 256
 HALF = 128
 CHUNK = 8
+UNROLL = 4
+AHEAD = 0
 NB = 3
 F32 = jnp.float32
 BF16 = jnp.bfloat16
@@ -128,7 +130,7 @@
     return jnp.broadcast_to(ref[pl.ds(at, 1), :], (16, ref.shape[1])).astype(BF16)
 
 
-def prepare(code_ref, hi_ref, sign_ref, lo_ref, hot_ref, count_ref):
+def unpack_codes(code_ref, hi_ref, sign_ref, lo_ref):
     codes = code_ref[...].reshape(INPUTS, INPUTS).astype(jnp.int32)
     row = lax.broadcasted_iota(jnp.int32, (HALF, HALF), 0)
     col = lax.broadcasted_iota(jnp.int32, (HALF, HALF), 1)
@@ -140,29 +142,45 @@
     sign_ref[...] = jnp.where(code >= 0, 1.0, -1.0).astype(F32)
     hi_ref[...] = lax.shift_right_logical(target, 7).astype(F32)
     lo_ref[...] = jnp.where(col != row, target & 127, -1).astype(F32)
+
+
+def row_ids():
     sub = lax.broadcasted_iota(jnp.int32, (16, INPUTS), 0)
-    rows = [(sub + r * 16).astype(F32).astype(BF16) for r in range(8)]
+    return [(sub + r * 16).astype(F32).astype(BF16) for r in range(8)]
+
+
+def one_hot(lo_ref, at, rows):
+    one, zero = jnp.ones((), BF16), jnp.zeros((), BF16)
+    lo = packed_row(lo_ref, at)
+    return jnp.concatenate([jnp.where(lo == rows[r], one, zero) for r in range(8)], axis=0)
+
+
+def prepare(lo_ref, hot_ref):
+    rows = row_ids()
+
+    @pl.loop(0, AHEAD * UNROLL)
+    def _(step):
+        for n in range(CHUNK):
+            hot = one_hot(lo_ref, step * CHUNK + n, rows)
+            hot_ref[step, 256 * n : 256 * n + 128, :] = hot[:, :128]
+            hot_ref[step, 256 * n + 128 : 256 * n + 256, :] = hot[:, 128:]
+
+
+def count_pairs(hi_ref, lo_ref, count_ref):
+    rows = row_ids()
     one, zero = jnp.ones((), BF16), jnp.zeros((), BF16)
     count_ref[...] = jnp.zeros_like(count_ref)
 
     @pl.loop(0, HALF // CHUNK)
     def _(step):
-        marks = []
-        hots = []
-        for n in range(CHUNK):
-            lo = packed_row(lo_ref, step * CHUNK + n)
-            hi = packed_row(hi_ref, step * CHUNK + n)
-            hot = jnp.concatenate([jnp.where(lo == rows[r], one, zero) for r in range(8)], axis=0)
-            hot_ref[step, 2 * n] = hot[:, :128]
-            hot_ref[step, 2 * n + 1] = hot[:, 128:]
-            hots.append(hot)
-            marks.append(jnp.where(hi == rows[0], one, zero))
+        hots = [one_hot(lo_ref, step * CHUNK + n, rows) for n in range(CHUNK)]
+        marks = [jnp.where(packed_row(hi_ref, step * CHUNK + n) == rows[0], one, zero) for n in range(CHUNK)]
         hot = jnp.concatenate(hots, axis=1)
         mark = jnp.concatenate(marks, axis=1)
         count_ref[...] += lax.dot_general(mark, hot, NT, preferred_element_type=F32)
 
 
-def stack_pairs(x_ref, hi_ref, sign_ref, hot_ref, xf_ref, data_a, data_b, acc_ref):
+def stack_pairs(x_ref, hi_ref, sign_ref, lo_ref, hot_ref, xf_ref, acc_ref):
     x = x_ref[...].reshape(INPUTS, 128)
     xf = x.astype(F32)
     xf_ref[0] = xf
@@ -174,7 +192,9 @@
     lane_j = lax.broadcasted_iota(jnp.int32, (32, 128), 1)
     zero = jnp.zeros((), BF16)
 
-    def produce(step, data_ref):
+    ids = row_ids()
+
+    def produce(step, ready):
         base = step * CHUNK
         left, right = [], []
         for n in range(CHUNK):
@@ -186,46 +206,50 @@
         x = x_ref[...].reshape(INPUTS, 128)
         one = lax.dot_general(left, x, NT, preferred_element_type=F32)
         two = lax.dot_general(right, x[HALF:], NT, preferred_element_type=F32)
+        data = []
         for n in range(CHUNK):
             at = slice(n * 32, n * 32 + 32)
             low = jnp.where(lane_j > base + n, one[at, :128], two[at, :])
             both = jnp.concatenate([low, one[at, 128:]], axis=1).astype(BF16)
             hi = packed_row(hi_ref, base + n)
             sign = packed_row(sign_ref, base + n)
-            real = both[:16]
-            imag = both[16:] * sign
+            parts = []
             for b in range(NB):
                 mine = hi == jnp.full((16, INPUTS), b, BF16)
-                re = jnp.where(mine, real, zero)
-                im = jnp.where(mine, imag, zero)
-                for h in range(2):
-                    half = slice(h * 128, h * 128 + 128)
-                    data_ref[2 * n + h, b * 32 : b * 32 + 16, :] = re[:, half]
-                    data_ref[2 * n + h, b * 32 + 16 : b * 32 + 32, :] = im[:, half]
-
-    def consume(step, data_ref):
-        data = jnp.concatenate([data_ref[m] for m in range(2 * CHUNK)], axis=1)
-        hot = jnp.concatenate([hot_ref[step, m] for m in range(2 * CHUNK)], axis=1)
-        acc_ref[...] += lax.dot_general(data, hot, NT, preferred_element_type=F32)
-
-    steps = HALF // CHUNK
-    produce(0, data_a)
-
-    @pl.loop(0, steps // 2)
-    def _(k):
-        produce(2 * k + 1, data_b)
-        consume(2 * k, data_a)
-        produce(jnp.minimum(2 * k + 2, steps - 1), data_a)
-        consume(2 * k + 1, data_b)
-
-
-def messages(acc_ref, count_ref, perm_ref, send_ref):
-    parts = []
-    for b in range(NB):
-        parts.append(acc_ref[b * 32 : b * 32 + 32, :] / jnp.maximum(count_ref[b : b + 1, :], 1.0))
-    means = jnp.concatenate(parts, axis=1).astype(BF16)
+                parts.append(jnp.where(mine, both[:16], zero))
+                parts.append(jnp.where(mine, both[16:] * sign, zero))
+            data.append(jnp.concatenate(parts, axis=0))
+        if ready:
+            hot = [hot_ref[step, m * 128 : m * 128 + 128] for m in range(2 * CHUNK)]
+        else:
+            hot = [one_hot(lo_ref, base + n, ids) for n in range(CHUNK)]
+        return data, hot
+
+    def product(data, hot):
+        data = jnp.concatenate(data, axis=1)
+        hot = jnp.concatenate(hot, axis=1)
+        return lax.dot_general(data, hot, NT, preferred_element_type=F32)
+
+    def sweep(first, last, ready):
+        @pl.loop(first, last)
+        def _(k):
+            data, hot = [], []
+            for u in range(UNROLL):
+                d, h = produce(k * UNROLL + u, ready)
+                data += d
+                hot += h
+            acc_ref[...] += product(data, hot)
+
+    if AHEAD:
+        sweep(0, AHEAD, True)
+    if AHEAD < HALF // CHUNK // UNROLL:
+        sweep(AHEAD, HALF // CHUNK // UNROLL, False)
+
+
+def messages(acc_ref, perm_ref, send_ref):
+    sums = jnp.concatenate([acc_ref[b * 32 : b * 32 + 32, :] for b in range(NB)], axis=1).astype(BF16)
     perm = perm_ref[...].reshape(FEEDS * 64, NB * 128)
-    out = lax.dot_general(means, perm, NT, preferred_element_type=F32)
+    out = lax.dot_general(sums, perm, NT, preferred_element_type=F32)
     first = lax.broadcasted_iota(jnp.int32, (16, 128), 1) < 64
     for o in range(0, FEEDS, 2):
         real = out[:16, o * 64 : o * 64 + 128]
@@ -234,11 +258,21 @@
         send_ref[o + 1] = jnp.where(first, pltpu.roll(real, 64, 1), imag).astype(BF16)
 
 
-def finish(block, out_ref):
+def slot_scale(count_ref, perm):
+    count = jnp.concatenate([count_ref[b : b + 1, :] for b in range(NB)], axis=1)
+    high = jnp.floor(count * (1.0 / 256.0))
+    digit = lax.broadcasted_iota(jnp.int32, (16, NB * 128), 0)
+    digits = jnp.where(digit == 0, high, count - 256.0 * high).astype(BF16)
+    got = lax.dot_general(perm, digits, NT, preferred_element_type=F32)
+    return 1.0 / jnp.maximum(256.0 * got[:, 0:1] + got[:, 1:2], 1.0)
+
+
+def finish(block, scale, out_ref):
     turned = jnp.transpose(block.astype(F32))
     for h in range(2):
         for q in range(2):
-            out_ref[pl.ds(2 * h + q, CAP, stride=4), :] = turned[q * 64 : q * 64 + CAP, h * 128 : h * 128 + 128]
+            mean = turned[q * 64 : q * 64 + CAP, h * 128 : h * 128 + 128] * scale[:CAP]
+            out_ref[pl.ds(2 * h + q, CAP, stride=4), :] = mean
 
 
 def far_first(axis):
@@ -296,17 +330,20 @@
     x_ref, win_ref, first_ref, tw_ref, second_ref, owner_ref, raw_code,
     mixed_ref, wide_ref, wsend, wrecv, bsend, spec_ref, code_ref,
     hi_ref, sign_ref, lo_ref, hot_ref, perm_ref, count_ref,
-    xf_ref, data_a, data_b, acc_ref, msend, mrecv,
-    local_sem, wss, wrs, css, crs, bss, brs, mss, mrs,
+    xf_ref, acc_ref, msend, mrecv,
+    known, local_sem, wss, wrs, css, crs, bss, brs, mss, mrs,
 ):
     feed = lax.axis_index("feed")
     chan = lax.axis_index("chan")
+    z, yc = feed // 4, lax.rem(feed, 4)
+    y, c = yc // 2, lax.rem(yc, 2)
+    along_z = [{"feed": lax.rem(z + d, 4) * 4 + yc} for d in (2, 1, 3)]
+    along_yc = [
+        {"feed": z * 4 + lax.rem(y + e, 2) * 2 + lax.rem(c + d, 2)} for e, d in ((1, 1), (1, 0), (0, 1))
+    ]
     barrier = pltpu.get_barrier_semaphore()
-    for axis in ("chan", "feed"):
-        for peer in peers(axis):
-            pl.semaphore_signal(
-                barrier, inc=1, device_id={axis: peer}, device_id_type=pl.DeviceIdType.MESH
-            )
+    for device in [{"chan": peer} for peer in peers("chan")] + along_z + along_yc:
+        pl.semaphore_signal(barrier, inc=1, device_id=device, device_id_type=pl.DeviceIdType.MESH)
     loads = [
         pltpu.make_async_copy(a, b, local_sem.at[n])
         for n, (a, b) in enumerate([
@@ -322,23 +359,29 @@
     wsend[...] = wide.reshape(GROUPS, 32, 128)
     code_ref[feed] = raw_code[...].astype(jnp.int16)
     permutation(owner_ref, perm_ref)
-    pl.semaphore_wait(barrier, GROUPS + FEEDS - 2)
+    pl.semaphore_wait(barrier, 13)
+    for device in along_z:
+        pl.semaphore_signal(known, inc=1, device_id=device, device_id_type=pl.DeviceIdType.MESH)
     w_arrived, w_sent = exchange(lambda d: wsend.at[d], wrecv, wss, wrs, "chan")
+    wrecv[chan] = wsend[chan]
+    pl.semaphore_wait(known, 3)
     c_arrived, c_sent = exchange(lambda d: code_ref.at[feed], code_ref, css, crs, "feed")
-    wrecv[chan] = wsend[chan]
     w_arrived()
     bsend[...] = regroup(wrecv[...].reshape(256, 128)).reshape(FEEDS, 16, 128)
     b_arrived, b_sent = exchange(lambda d: bsend.at[d], spec_ref, bss, brs, "feed")
     spec_ref[feed] = bsend[feed]
     c_arrived()
-    prepare(code_ref, hi_ref, sign_ref, lo_ref, hot_ref, count_ref)
+    unpack_codes(code_ref, hi_ref, sign_ref, lo_ref)
+    prepare(lo_ref, hot_ref)
     b_arrived()
-    stack_pairs(spec_ref, hi_ref, sign_ref, hot_ref, xf_ref, data_a, data_b, acc_ref)
-    messages(acc_ref, count_ref, perm_ref, msend)
+    stack_pairs(spec_ref, hi_ref, sign_ref, lo_ref, hot_ref, xf_ref, acc_ref)
+    messages(acc_ref, perm_ref, msend)
     m_arrived, m_sent = exchange(lambda d: msend.at[d], mrecv, mss, mrs, "feed")
     mrecv[feed] = msend[feed]
+    count_pairs(hi_ref, lo_ref, count_ref)
+    scale = slot_scale(count_ref, perm_ref[feed])
     m_arrived()
-    finish(mrecv[...].reshape(256, 128), out_ref)
+    finish(mrecv[...].reshape(256, 128), scale, out_ref)
     w_sent()
     c_sent()
     b_sent()
@@ -374,15 +417,14 @@
             pltpu.VMEM((HALF, INPUTS), F32),
             pltpu.VMEM((HALF, INPUTS), F32),
             pltpu.VMEM((HALF, INPUTS), F32),
-            pltpu.VMEM((HALF // CHUNK, 2 * CHUNK, 128, 128), BF16),
+            pltpu.VMEM((HALF // CHUNK, 2 * CHUNK * 128, 128), BF16),
             pltpu.VMEM((FEEDS, 64, NB * 128), BF16),
             pltpu.VMEM((16, 128), F32),
             pltpu.VMEM((2, INPUTS, 128), F32),
-            pltpu.VMEM((2 * CHUNK, rows, 128), BF16),
-            pltpu.VMEM((2 * CHUNK, rows, 128), BF16),
             pltpu.VMEM((rows, 128), F32),
             pltpu.VMEM((FEEDS, 16, 128), BF16),
             pltpu.VMEM((FEEDS, 16, 128), BF16),
+            pltpu.SemaphoreType.REGULAR,
             dma((7,)),
             dma, dma, dma, dma, dma, dma, dma, dma,
         ],

time: 30 us -> 28.6 us (0.953)
  Pallas kernels: 28.3 us -> 26.8 us
    pallas_call x1, Pallas kernels: 28.3 us -> 26.8 us  [per_device(): pl.pallas_call(kernel, out_shape=jax.ShapeDtypeStruct((4 * CAP, 128), F32...]
where the time goes in v4:
time: 28.6 us; the launch traced here: 28.4 us
  Pallas kernels  26.8 us (94%)
  local copies, waits for them, and re-layouts  1.59 us (6%)
    pallas_call x1, Pallas kernels, per_device(): pl.pallas_call(kernel, out_shape=jax.ShapeDtypeStruct((4 * CAP, 128), F32...  26.8 us
    reshape x1, local copies, waits for them, and re-layouts, per_device(): turned.reshape(CAP, 2, 2, 128).transpose(0, 2, 1, 3).reshape(CAP, 2, 256)  1.59 us

profile of v4, /device:TPU:1, one launch (start us, length us, event | category | flops | bytes accessed | tf_op | source)
XLA Modules:
  0.0 28.4 jit_solution(8605540874821254891)
XLA Ops:
  0.0 26.8 %shard_map.73 = f32[188,128]{1,0:T(8,128)} custom-call(bf16[1408,128]{1,0:T(8,128)(2,1)} %bitcast.8, f32[8,128,128]{2,1,0:T(8,128)} %constant.8.clone.win_hbm, bf16[256,128]{1,0:T(8,128)(2,1)} %constant.13.first_hbm, f32[2,128,128]{2,1,0:T(8,128)} %constant.10.clone.tw_hbm, bf16[32,256]{1,0:T(8,128)(2,1)} %constant.14.second_hbm, s32[16,256]{1,0:T(8,128)} %code_hbm.1, ...), custom_call_target="tpu_custom_call" | custom-call | tf_op jit(solution)/shard_map/pallas_call | solution.py:397
  26.8 1.6 %reshape.14 = f32[47,2,2,128]{3,2,1,0:T(2,128)} reshape(f32[188,128]{1,0:T(8,128)} %shard_map.73) | data formatting | bytes 192512 | tf_op jit(solution)/shard_map/reshape | solution.py:435

commit v5 on v4

--- a/solution.py
+++ b/solution.py
@@ -19,9 +19,9 @@
 GROUPS = 8
 INPUTS = 256
 HALF = 128
-CHUNK = 8
-UNROLL = 4
-AHEAD = 0
+CHUNK = 16
+UNROLL = 8
+EARLY = 4
 NB = 3
 F32 = jnp.float32
 BF16 = jnp.bfloat16
@@ -155,23 +155,11 @@
     return jnp.concatenate([jnp.where(lo == rows[r], one, zero) for r in range(8)], axis=0)
 
 
-def prepare(lo_ref, hot_ref):
-    rows = row_ids()
-
-    @pl.loop(0, AHEAD * UNROLL)
-    def _(step):
-        for n in range(CHUNK):
-            hot = one_hot(lo_ref, step * CHUNK + n, rows)
-            hot_ref[step, 256 * n : 256 * n + 128, :] = hot[:, :128]
-            hot_ref[step, 256 * n + 128 : 256 * n + 256, :] = hot[:, 128:]
-
-
-def count_pairs(hi_ref, lo_ref, count_ref):
+def count_pairs(first, last, hi_ref, lo_ref, count_ref):
     rows = row_ids()
     one, zero = jnp.ones((), BF16), jnp.zeros((), BF16)
-    count_ref[...] = jnp.zeros_like(count_ref)
-
-    @pl.loop(0, HALF // CHUNK)
+
+    @pl.loop(first, last)
     def _(step):
         hots = [one_hot(lo_ref, step * CHUNK + n, rows) for n in range(CHUNK)]
         marks = [jnp.where(packed_row(hi_ref, step * CHUNK + n) == rows[0], one, zero) for n in range(CHUNK)]
@@ -180,7 +168,7 @@
         count_ref[...] += lax.dot_general(mark, hot, NT, preferred_element_type=F32)
 
 
-def stack_pairs(x_ref, hi_ref, sign_ref, lo_ref, hot_ref, xf_ref, acc_ref):
+def stack_pairs(x_ref, hi_ref, sign_ref, lo_ref, xf_ref, acc_ref):
     x = x_ref[...].reshape(INPUTS, 128)
     xf = x.astype(F32)
     xf_ref[0] = xf
@@ -194,7 +182,7 @@
 
     ids = row_ids()
 
-    def produce(step, ready):
+    def produce(step):
         base = step * CHUNK
         left, right = [], []
         for n in range(CHUNK):
@@ -219,35 +207,27 @@
                 parts.append(jnp.where(mine, both[:16], zero))
                 parts.append(jnp.where(mine, both[16:] * sign, zero))
             data.append(jnp.concatenate(parts, axis=0))
-        if ready:
-            hot = [hot_ref[step, m * 128 : m * 128 + 128] for m in range(2 * CHUNK)]
-        else:
-            hot = [one_hot(lo_ref, base + n, ids) for n in range(CHUNK)]
+        hot = [one_hot(lo_ref, base + n, ids) for n in range(CHUNK)]
         return data, hot
 
     def product(data, hot):
         data = jnp.concatenate(data, axis=1)
         hot = jnp.concatenate(hot, axis=1)
-        return lax.dot_general(data, hot, NT, preferred_element_type=F32)
-
-    def sweep(first, last, ready):
-        @pl.loop(first, last)
-        def _(k):
-            data, hot = [], []
-            for u in range(UNROLL):
-                d, h = produce(k * UNROLL + u, ready)
-                data += d
-                hot += h
-            acc_ref[...] += product(data, hot)
-
-    if AHEAD:
-        sweep(0, AHEAD, True)
-    if AHEAD < HALF // CHUNK // UNROLL:
-        sweep(AHEAD, HALF // CHUNK // UNROLL, False)
+        return lax.dot_general(hot, data, NT, preferred_element_type=F32)
+
+    @pl.loop(0, HALF // CHUNK // UNROLL)
+    def _(k):
+        data, hot = [], []
+        for u in range(UNROLL):
+            d, h = produce(k * UNROLL + u)
+            data += d
+            hot += h
+        acc_ref[...] += product(data, hot)
 
 
 def messages(acc_ref, perm_ref, send_ref):
-    sums = jnp.concatenate([acc_ref[b * 32 : b * 32 + 32, :] for b in range(NB)], axis=1).astype(BF16)
+    turned = jnp.transpose(jnp.concatenate([acc_ref[...], jnp.zeros((128, 32), F32)], axis=1))
+    sums = jnp.concatenate([turned[b * 32 : b * 32 + 32, :] for b in range(NB)], axis=1).astype(BF16)
     perm = perm_ref[...].reshape(FEEDS * 64, NB * 128)
     out = lax.dot_general(sums, perm, NT, preferred_element_type=F32)
     first = lax.broadcasted_iota(jnp.int32, (16, 128), 1) < 64
@@ -329,7 +309,7 @@
     x_hbm, win_hbm, first_hbm, tw_hbm, second_hbm, code_hbm, owner_hbm, out_ref,
     x_ref, win_ref, first_ref, tw_ref, second_ref, owner_ref, raw_code,
     mixed_ref, wide_ref, wsend, wrecv, bsend, spec_ref, code_ref,
-    hi_ref, sign_ref, lo_ref, hot_ref, perm_ref, count_ref,
+    hi_ref, sign_ref, lo_ref, perm_ref, count_ref,
     xf_ref, acc_ref, msend, mrecv,
     known, local_sem, wss, wrs, css, crs, bss, brs, mss, mrs,
 ):
@@ -372,13 +352,14 @@
     spec_ref[feed] = bsend[feed]
     c_arrived()
     unpack_codes(code_ref, hi_ref, sign_ref, lo_ref)
-    prepare(lo_ref, hot_ref)
+    count_ref[...] = jnp.zeros_like(count_ref)
+    count_pairs(0, EARLY, hi_ref, lo_ref, count_ref)
     b_arrived()
-    stack_pairs(spec_ref, hi_ref, sign_ref, lo_ref, hot_ref, xf_ref, acc_ref)
+    stack_pairs(spec_ref, hi_ref, sign_ref, lo_ref, xf_ref, acc_ref)
     messages(acc_ref, perm_ref, msend)
     m_arrived, m_sent = exchange(lambda d: msend.at[d], mrecv, mss, mrs, "feed")
     mrecv[feed] = msend[feed]
-    count_pairs(hi_ref, lo_ref, count_ref)
+    count_pairs(EARLY, HALF // CHUNK, hi_ref, lo_ref, count_ref)
     scale = slot_scale(count_ref, perm_ref[feed])
     m_arrived()
     finish(mrecv[...].reshape(256, 128), scale, out_ref)
@@ -417,11 +398,10 @@
             pltpu.VMEM((HALF, INPUTS), F32),
             pltpu.VMEM((HALF, INPUTS), F32),
             pltpu.VMEM((HALF, INPUTS), F32),
-            pltpu.VMEM((HALF // CHUNK, 2 * CHUNK * 128, 128), BF16),
             pltpu.VMEM((FEEDS, 64, NB * 128), BF16),
             pltpu.VMEM((16, 128), F32),
             pltpu.VMEM((2, INPUTS, 128), F32),
-            pltpu.VMEM((rows, 128), F32),
+            pltpu.VMEM((128, rows), F32),
             pltpu.VMEM((FEEDS, 16, 128), BF16),
             pltpu.VMEM((FEEDS, 16, 128), BF16),
             pltpu.SemaphoreType.REGULAR,

time: 28.6 us -> 26.8 us (0.937)
  Pallas kernels: 26.8 us -> 25.1 us
    pallas_call x1, Pallas kernels: 26.8 us -> 25.1 us  [per_device(): pl.pallas_call(kernel, out_shape=jax.ShapeDtypeStruct((4 * CAP, 128), F32...]
where the time goes in v5:
time: 26.8 us; the launch traced here: 26.7 us
  Pallas kernels  25.1 us (94%)
  local copies, waits for them, and re-layouts  1.59 us (6%)
    pallas_call x1, Pallas kernels, per_device(): pl.pallas_call(kernel, out_shape=jax.ShapeDtypeStruct((4 * CAP, 128), F32...  25.1 us
    reshape x1, local copies, waits for them, and re-layouts, per_device(): turned.reshape(CAP, 2, 2, 128).transpose(0, 2, 1, 3).reshape(CAP, 2, 256)  1.59 us

profile of v5, /device:TPU:1, one launch (start us, length us, event | category | flops | bytes accessed | tf_op | source)
XLA Modules:
  0.0 26.7 jit_solution(16512414958843003984)
XLA Ops:
  0.0 25.1 %shard_map.73 = f32[188,128]{1,0:T(8,128)} custom-call(bf16[1408,128]{1,0:T(8,128)(2,1)} %bitcast.8, f32[8,128,128]{2,1,0:T(8,128)} %constant.8.clone.win_hbm, bf16[256,128]{1,0:T(8,128)(2,1)} %constant.13.first_hbm, f32[2,128,128]{2,1,0:T(8,128)} %constant.10.clone.tw_hbm, bf16[32,256]{1,0:T(8,128)(2,1)} %constant.14.second_hbm, s32[16,256]{1,0:T(8,128)} %code_hbm.1, ...), custom_call_target="tpu_custom_call" | custom-call | tf_op jit(solution)/shard_map/pallas_call | solution.py:378
  25.1 1.6 %reshape.14 = f32[47,2,2,128]{3,2,1,0:T(2,128)} reshape(f32[188,128]{1,0:T(8,128)} %shard_map.73) | data formatting | bytes 192512 | tf_op jit(solution)/shard_map/reshape | solution.py:415

commit v6 on v5

--- a/solution.py
+++ b/solution.py
@@ -99,12 +99,11 @@
     return wide_ref[...].astype(BF16)
 
 
-def regroup(block):
+def regroup_matrix():
     row = lax.broadcasted_iota(jnp.int32, (256, 256), 0)
     col = lax.broadcasted_iota(jnp.int32, (256, 256), 1)
     source = ((row // 2) % 8) * 32 + (row // 16) * 2 + row % 2
-    take = jnp.where(col == source, 1.0, 0.0).astype(BF16)
-    return jnp.dot(take, block, preferred_element_type=F32).astype(BF16)
+    return jnp.where(col == source, 1.0, 0.0).astype(BF16)
 
 
 def permutation(owner_ref, perm_ref):
@@ -311,7 +310,7 @@
     mixed_ref, wide_ref, wsend, wrecv, bsend, spec_ref, code_ref,
     hi_ref, sign_ref, lo_ref, perm_ref, count_ref,
     xf_ref, acc_ref, msend, mrecv,
-    known, local_sem, wss, wrs, css, crs, bss, brs, mss, mrs,
+    take_ref, known, local_sem, wss, wrs, css, crs, bss, brs, mss, mrs,
 ):
     feed = lax.axis_index("feed")
     chan = lax.axis_index("chan")
@@ -339,6 +338,7 @@
     wsend[...] = wide.reshape(GROUPS, 32, 128)
     code_ref[feed] = raw_code[...].astype(jnp.int16)
     permutation(owner_ref, perm_ref)
+    take_ref[...] = regroup_matrix()
     pl.semaphore_wait(barrier, 13)
     for device in along_z:
         pl.semaphore_signal(known, inc=1, device_id=device, device_id_type=pl.DeviceIdType.MESH)
@@ -347,7 +347,8 @@
     pl.semaphore_wait(known, 3)
     c_arrived, c_sent = exchange(lambda d: code_ref.at[feed], code_ref, css, crs, "feed")
     w_arrived()
-    bsend[...] = regroup(wrecv[...].reshape(256, 128)).reshape(FEEDS, 16, 128)
+    regrouped = jnp.dot(take_ref[...], wrecv[...].reshape(256, 128), preferred_element_type=F32)
+    bsend[...] = regrouped.astype(BF16).reshape(FEEDS, 16, 128)
     b_arrived, b_sent = exchange(lambda d: bsend.at[d], spec_ref, bss, brs, "feed")
     spec_ref[feed] = bsend[feed]
     c_arrived()
@@ -377,7 +378,7 @@
     dma = pltpu.SemaphoreType.DMA
     turned = pl.pallas_call(
         kernel,
-        out_shape=jax.ShapeDtypeStruct((4 * CAP, 128), F32),
+        out_shape=pltpu.VMEM((4 * CAP, 128), F32),
         in_specs=[pl.BlockSpec(memory_space=pl.ANY)] * 7,
         out_specs=pl.BlockSpec(memory_space=pltpu.VMEM),
         scratch_shapes=[
@@ -404,6 +405,7 @@
             pltpu.VMEM((128, rows), F32),
             pltpu.VMEM((FEEDS, 16, 128), BF16),
             pltpu.VMEM((FEEDS, 16, 128), BF16),
+            pltpu.VMEM((256, 256), BF16),
             pltpu.SemaphoreType.REGULAR,
             dma((7,)),
             dma, dma, dma, dma, dma, dma, dma, dma,

time: 26.8 us -> 25.3 us (0.944)
  local copies, waits for them, and re-layouts: 1.59 us -> 0.69 us
  Pallas kernels: 25.1 us -> 24.4 us
    reshape x1, local copies, waits for them, and re-layouts: 1.59 us -> 0.69 us  [per_device(): turned.reshape(CAP, 2, 2, 128).transpose(0, 2, 1, 3).reshape(CAP, 2, 256)]
    pallas_call x1, Pallas kernels: 25.1 us -> 24.4 us  [per_device(): pl.pallas_call(kernel, out_shape=pltpu.VMEM((4 * CAP, 128), F32), in_spec...]
where the time goes in v6:
time: 25.3 us; the launch traced here: 25.1 us
  Pallas kernels  24.4 us (96%)
  local copies, waits for them, and re-layouts  0.69 us (3%)
    pallas_call x1, Pallas kernels, per_device(): pl.pallas_call(kernel, out_shape=pltpu.VMEM((4 * CAP, 128), F32), in_spec...  24.4 us
    reshape x1, local copies, waits for them, and re-layouts, per_device(): turned.reshape(CAP, 2, 2, 128).transpose(0, 2, 1, 3).reshape(CAP, 2, 256)  0.69 us

profile of v6, /device:TPU:1, one launch (start us, length us, event | category | flops | bytes accessed | tf_op | source)
XLA Modules:
  0.0 25.1 jit_solution(3727430735330421904)
XLA Ops:
  0.0 24.4 %shard_map.73 = f32[188,128]{1,0:T(8,128)S(1)} custom-call(bf16[1408,128]{1,0:T(8,128)(2,1)} %bitcast.8, f32[8,128,128]{2,1,0:T(8,128)} %constant.8.clone.win_hbm, bf16[256,128]{1,0:T(8,128)(2,1)} %constant.13.first_hbm, f32[2,128,128]{2,1,0:T(8,128)} %constant.10.clone.tw_hbm, bf16[32,256]{1,0:T(8,128)(2,1)} %constant.14.second_hbm, s32[16,256]{1,0:T(8,128)} %code_hbm.1, ...), custom_call_target="tpu_custom_call" | custom-call | tf_op jit(solution)/shard_map/pallas_call | solution.py:379
  24.4 0.7 %reshape.14 = f32[47,2,2,128]{3,2,1,0:T(2,128)} reshape(f32[188,128]{1,0:T(8,128)S(1)} %shard_map.73) | data formatting | bytes 192512 | tf_op jit(solution)/shard_map/reshape | solution.py:417

commit v7 on v6

--- a/solution.py
+++ b/solution.py
@@ -176,7 +176,7 @@
     lane = lax.broadcasted_iota(jnp.int32, (16, 128), 1)
     sub = lax.broadcasted_iota(jnp.int32, (16, 128), 0)
     pick = jnp.where(lane % 16 == sub, 1.0, 0.0).astype(BF16)
-    lane_j = lax.broadcasted_iota(jnp.int32, (32, 128), 1)
+    lane_j = lax.broadcasted_iota(jnp.int32, (32, 128), 1).astype(F32).astype(BF16)
     zero = jnp.zeros((), BF16)
 
     ids = row_ids()
@@ -196,8 +196,9 @@
         data = []
         for n in range(CHUNK):
             at = slice(n * 32, n * 32 + 32)
-            low = jnp.where(lane_j > base + n, one[at, :128], two[at, :])
-            both = jnp.concatenate([low, one[at, 128:]], axis=1).astype(BF16)
+            above = lane_j > (base + n).astype(F32).astype(BF16)
+            low = jnp.where(above, one[at, :128].astype(BF16), two[at, :].astype(BF16))
+            both = jnp.concatenate([low, one[at, 128:].astype(BF16)], axis=1)
             hi = packed_row(hi_ref, base + n)
             sign = packed_row(sign_ref, base + n)
             parts = []

time: 25.3 us -> 25.3 us (level)
  no operation moved by 1% of the time
where the time goes in v7:
time: 25.3 us; the launch traced here: 25.2 us
  Pallas kernels  24.5 us (97%)
  local copies, waits for them, and re-layouts  0.69 us (3%)
    pallas_call x1, Pallas kernels, per_device(): pl.pallas_call(kernel, out_shape=pltpu.VMEM((4 * CAP, 128), F32), in_spec...  24.5 us
    reshape x1, local copies, waits for them, and re-layouts, per_device(): turned.reshape(CAP, 2, 2, 128).transpose(0, 2, 1, 3).reshape(CAP, 2, 256)  0.69 us

profile of v7, /device:TPU:1, one launch (start us, length us, event | category | flops | bytes accessed | tf_op | source)
XLA Modules:
  0.0 25.2 jit_solution(1388028274391442692)
XLA Ops:
  0.0 24.5 %shard_map.73 = f32[188,128]{1,0:T(8,128)S(1)} custom-call(bf16[1408,128]{1,0:T(8,128)(2,1)} %bitcast.8, f32[8,128,128]{2,1,0:T(8,128)} %constant.8.clone.win_hbm, bf16[256,128]{1,0:T(8,128)(2,1)} %constant.13.first_hbm, f32[2,128,128]{2,1,0:T(8,128)} %constant.10.clone.tw_hbm, bf16[32,256]{1,0:T(8,128)(2,1)} %constant.14.second_hbm, s32[16,256]{1,0:T(8,128)} %code_hbm.1, ...), custom_call_target="tpu_custom_call" | custom-call | tf_op jit(solution)/shard_map/pallas_call | solution.py:380
  24.5 0.7 %reshape.14 = f32[47,2,2,128]{3,2,1,0:T(2,128)} reshape(f32[188,128]{1,0:T(8,128)S(1)} %shard_map.73) | data formatting | bytes 192512 | tf_op jit(solution)/shard_map/reshape | solution.py:418

commit v8 on v7

--- a/solution.py
+++ b/solution.py
@@ -249,10 +249,8 @@
 
 def finish(block, scale, out_ref):
     turned = jnp.transpose(block.astype(F32))
-    for h in range(2):
-        for q in range(2):
-            mean = turned[q * 64 : q * 64 + CAP, h * 128 : h * 128 + 128] * scale[:CAP]
-            out_ref[pl.ds(2 * h + q, CAP, stride=4), :] = mean
+    for q in range(2):
+        out_ref[:, q, :] = turned[q * 64 : q * 64 + CAP] * scale[:CAP]
 
 
 def far_first(axis):
@@ -379,7 +377,7 @@
     dma = pltpu.SemaphoreType.DMA
     turned = pl.pallas_call(
         kernel,
-        out_shape=pltpu.VMEM((4 * CAP, 128), F32),
+        out_shape=pltpu.VMEM((CAP, 2, 256), F32),
         in_specs=[pl.BlockSpec(memory_space=pl.ANY)] * 7,
         out_specs=pl.BlockSpec(memory_space=pltpu.VMEM),
         scratch_shapes=[
@@ -415,7 +413,7 @@
             vmem_limit_bytes=60 << 20, collective_id=0, has_side_effects=True
         ),
     )(x, win, bf(first_matrix()), jnp.asarray(twiddle_tables()), bf(second_matrix()), stack_code, owner)
-    return turned.reshape(CAP, 2, 2, 128).transpose(0, 2, 1, 3).reshape(CAP, 2, 256)
+    return turned
 
 
 def solution(mesh):

time: 25.3 us -> 25.2 us (level)
    reshape x1 -> x0, local copies, waits for them, and re-layouts: 0.69 us -> none  [per_device(): turned.reshape(CAP, 2, 2, 128).transpose(0, 2, 1, 3).reshape(CAP, 2, 256)]
    unnamed x0 -> x1, local copies, waits for them, and re-layouts: none -> 0.64 us
where the time goes in v8:
time: 25.2 us; the launch traced here: 25.1 us
  Pallas kernels  24.5 us (97%)
  local copies, waits for them, and re-layouts  0.64 us (3%)
    pallas_call x1, Pallas kernels, per_device(): pl.pallas_call(kernel, out_shape=pltpu.VMEM((CAP, 2, 256), F32), in_specs...  24.5 us
    unnamed x1, local copies, waits for them, and re-layouts  0.64 us

profile of v8, /device:TPU:1, one launch (start us, length us, event | category | flops | bytes accessed | tf_op | source)
XLA Modules:
  0.0 25.1 jit_solution(195181554993265661)
XLA Ops:
  0.0 24.5 %shard_map.73 = f32[47,2,256]{2,1,0:T(2,128)S(1)} custom-call(bf16[1408,128]{1,0:T(8,128)(2,1)} %bitcast.5, f32[8,128,128]{2,1,0:T(8,128)} %constant.8.clone.win_hbm, bf16[256,128]{1,0:T(8,128)(2,1)} %constant.13.first_hbm, f32[2,128,128]{2,1,0:T(8,128)} %constant.10.clone.tw_hbm, bf16[32,256]{1,0:T(8,128)(2,1)} %constant.14.second_hbm, s32[16,256]{1,0:T(8,128)} %code_hbm.1, ...), custom_call_target="tpu_custom_call" | custom-call | tf_op jit(solution)/shard_map/pallas_call | solution.py:378
  24.5 0.6 %copy.10 = f32[47,2,256]{2,1,0:T(2,128)} copy(f32[47,2,256]{2,1,0:T(2,128)S(1)} %shard_map.73) | data formatting | bytes 192512
